TPU v7x, 256 devices: a whole 4x4x8 slice. The times are simulated.
256 devices in a mesh: ctx: 32 (over z, y_lo, core), tp: 8 (over x, y_hi).
Axes of the slice: x: 4, y: 4 (y_hi: 2, y_lo: 2; y = y_hi * 2 + y_lo), z: 8, core: 2. Of those that a mesh axis runs over, the one named last changes fastest.
Arguments:
- q_prompt: bfloat16 [8192, 7168], P('ctx', 'tp'), may hold values from -64 to 64
- kv_prompt: bfloat16 [8192, 8, 256], P('ctx', 'tp'), may hold values from -6 to 6
- q_ext: bfloat16 [2048, 7168], P('ctx', 'tp'), may hold values from -64 to 64
- kv_ext: bfloat16 [2048, 8, 256], P('ctx', 'tp'), may hold values from -6 to 6
- pool: bfloat16 [192, 128, 8, 256], P('ctx', None, 'tp'), may hold values from -6 to 6
- page_slot_table: int32 [144], replicated, may hold values from 0 to 191, as said below
Outputs:
- context: bfloat16 [10240, 7168], P(('ctx', 'tp'))
- pool_out: bfloat16 [192, 128, 8, 256], P('ctx', None, 'tp')
Inputs may be any that keep to these rules, and one draw needn't show every extreme that they name: `page_slot_table`: distinct slot numbers, one per page: entries 0 to 63 are the old cache's pages, then the extension's 16 pages in order, then the prompt's 64 pages in order; every block of 6 slots (slots c * 6 to (c + 1) * 6 - 1) holds exactly 2 old pages.
All inputs are finite; a program needn't handle non-finite values.
Results may differ from a plain program's by a relative error of at most 0.006.
Values may be sent and summed in bfloat16 or wider, within the bound.
No kernel may reach another device: no remote copies, remote signals or barrier semaphores. Data moves between devices by JAX's collectives and lax.ppermute only.
A program may use at most 64 MiB of HBM per device.

v0:
```python
import jax
import jax.numpy as jnp
from jax import lax
from jax.experimental import pallas as pl
from jax.experimental.pallas import tpu as pltpu
from jax.sharding import PartitionSpec as P

HEADS = 7
HD = 128
NEG = -1e30
C1 = 1.4426950408889634 * HD ** -0.5
F32 = jnp.float32
BF = jnp.bfloat16

VMEM = pl.BlockSpec(memory_space=pltpu.VMEM)
SMEM = pl.BlockSpec(memory_space=pltpu.SMEM)
ANY = pl.BlockSpec(memory_space=pl.ANY)
HBM = pl.BlockSpec(memory_space=pltpu.HBM)


def params():
    return pltpu.CompilerParams(vmem_limit_bytes=20 << 20)


def cost(flops, elems, nbytes):
    return pl.CostEstimate(flops=int(flops), transcendentals=int(elems), bytes_accessed=int(nbytes))


def update(q_ref, q0, state, rows, chunk, blocks, fix=None, source=None):
    source = state if source is None else source
    kv = blocks[0] if len(blocks) == 1 else jnp.concatenate(blocks, axis=0)
    keys = kv[:, :HD]
    values = jnp.concatenate([jnp.ones((kv.shape[0], HD), BF), kv[:, HD:]], axis=1)
    for r in range(0, rows, chunk):
        at = pl.ds(q0 + r, chunk)
        s = lax.dot_general(
            q_ref[at, :], keys, (((1,), (1,)), ((), ())), preferred_element_type=F32
        )
        if fix is not None:
            s = fix(s, r)
        m_old = source[at, :HD]
        m_new = jnp.maximum(m_old, jnp.max(s, axis=1, keepdims=True))
        p = jnp.exp2((s - jnp.concatenate([m_new] * (s.shape[1] // HD), axis=1)) * C1).astype(BF)
        alpha = jnp.exp2((m_old - m_new) * C1)
        pv = lax.dot_general(p, values, (((1,), (0,)), ((), ())), preferred_element_type=F32)
        state[at, :HD] = m_new
        state[at, HD:] = source[at, HD:] * jnp.concatenate([alpha, alpha], axis=1) + pv


def position(idx_ref):
    i = idx_ref[0]
    return i // 4, (i // 2) % 2, i % 2


def prep_body(idx_ref, table_ref, pool_ref, kvp_ref, kve_ref, qe_ref, x_ref, p_ref, sems):
    base = idx_ref[0] * 6

    def scan(j, found):
        n, a, b = found
        local = table_ref[j] - base
        inside = (local >= 0) & (local < 6)
        a = jnp.where(inside & (n == 0), local, a)
        b = jnp.where(inside & (n == 1), local, b)
        return n + inside.astype(jnp.int32), a, b

    zero = jnp.int32(0)
    early = [
        pltpu.make_async_copy(kvp_ref, x_ref.at[256:512], sems.at[0]),
        pltpu.make_async_copy(kve_ref, x_ref.at[512:576], sems.at[1]),
        pltpu.make_async_copy(kvp_ref, p_ref.at[0:256], sems.at[2]),
        pltpu.make_async_copy(kve_ref, p_ref.at[256:320], sems.at[3]),
    ]
    for h in range(HEADS):
        to = p_ref.at[320 + h // 2 * 64:384 + h // 2 * 64, h % 2 * HD:h % 2 * HD + HD]
        early.append(pltpu.make_async_copy(qe_ref.at[:, h * HD:(h + 1) * HD], to, sems.at[6 + h]))
    for copy in early:
        copy.start()
    _, a, b = lax.fori_loop(0, 64, scan, (zero, zero, zero))
    late = [
        pltpu.make_async_copy(pool_ref.at[a], x_ref.at[0:128], sems.at[4]),
        pltpu.make_async_copy(pool_ref.at[b], x_ref.at[128:256], sems.at[5]),
    ]
    for copy in late:
        copy.start()
    for copy in early + late:
        copy.wait()


def page_copies(idx_ref, table_ref, pool_ref, sems, items):
    base = idx_ref[0] * 6
    waits = []

    def add(entry, ref, row, count, to):
        local = table_ref[entry] - base
        go = (local >= 0) & (local < 6)
        sem = sems.at[len(waits)]

        def copy():
            return pltpu.make_async_copy(
                ref.at[row:row + count], pool_ref.at[local, pl.ds(to, count)], sem
            )

        @pl.when(go)
        def _():
            copy().start()

        waits.append((go, copy))

    for shard, ref, front, back, ext in items:
        if front is not None:
            add(80 + shard, ref, front, 128, 0)
        if back is not None:
            add(143 - shard, ref, back, 128, 0)
        if ext is not None:
            add(64 + shard // 2, ref, ext, 64, pl.multiple_of(shard % 2 * 64, 64))

    def wait():
        for go, copy in waits:
            @pl.when(go)
            def _(copy=copy):
                copy().wait()

    return wait


def shard_at(idx_ref, plane):
    return 4 * plane + idx_ref[0] % 4


def ext_plane(z, plane, qx_ref, se_ref, kv):
    bias = jnp.full((1, 128), jnp.where(plane < z, 0.0, NEG), F32)

    def fix(s, _):
        return jnp.concatenate([s[:, :512], s[:, 512:] + bias], axis=1)

    update(qx_ref, 0, se_ref, 896, 448, [kv[...]], fix)


def ext_planes(z, minus, plus, qx_ref, se_ref, kv_ref, parts):
    for i, (r, rc) in enumerate(parts):
        kv_ref[i, 0:256, :] = r[0:256, :]
        kv_ref[i, 256:512, :] = rc[0:256, :]
        kv_ref[i, 512:576, :] = r[512:576, :]
        kv_ref[i, 576:640, :] = rc[512:576, :]

    def one(i, carry):
        ext_plane(z, jnp.where(i == 0, minus, plus), qx_ref, se_ref, kv_ref.at[i])
        return carry

    lax.fori_loop(0, 2, one, 0)


def first_body(
    idx_ref, table_ref, qp_ref, qe_ref, x_ref, xc_ref, y_ref, yc_ref, a_ref, ac_ref, b_ref, bc_ref, pool_ref,
    qs_ref, qx_ref, sp_ref, se_ref, out_ref, token_ref, kv_ref, sems,
):
    z, y, c = position(idx_ref)
    j = 2 * y + c
    whole = pltpu.make_async_copy(pool_ref, out_ref, sems.at[24])
    whole.start()
    for h in range(HEADS):
        cols = slice(h * HD, (h + 1) * HD)
        qs_ref[h * 128:(h + 1) * 128, :] = qp_ref[0:128, cols]
        qs_ref[896 + h * 128:896 + (h + 1) * 128, :] = qp_ref[128:256, cols]
        qx_ref[h * 64:(h + 1) * 64, :] = qe_ref[:, cols]
        qx_ref[448 + h * 64:448 + (h + 1) * 64, :] = y_ref[320 + h // 2 * 64:384 + h // 2 * 64, h % 2 * HD:h % 2 * HD + HD]
    for state in (sp_ref, se_ref):
        state[:, :HD] = jnp.full((state.shape[0], HD), NEG, F32)
        state[:, HD:] = jnp.zeros((state.shape[0], 2 * HD), F32)
    whole.wait()
    minus = (z + 7) % 8
    plus = (z + 1) % 8
    own = idx_ref[0]
    am, bm = shard_at(idx_ref, minus), shard_at(idx_ref, plus)
    wait = page_copies(
        idx_ref, table_ref, out_ref, sems,
        [
            (own, x_ref, 256, 384, 512), (own ^ 1, xc_ref, 256, 384, 512),
            (own ^ 2, y_ref, 0, 128, 256), (own ^ 3, yc_ref, 0, 128, 256),
            (am, a_ref, 256, 384, 512), (am ^ 1, ac_ref, 256, 384, 512),
            (bm, b_ref, 256, 384, 512), (bm ^ 1, bc_ref, 256, 384, 512),
        ],
    )

    def shown(seen, width):
        return jnp.full((1, width), jnp.where(seen, 0.0, NEG), F32)

    rows = lax.broadcasted_iota(jnp.int32, (128, 128), 0)
    lanes = lax.broadcasted_iota(jnp.int32, (128, 128), 1)
    causal = jnp.where(rows >= lanes, 0.0, NEG).astype(F32)
    others = (j ^ 1, j ^ 2, j ^ 3)
    front = jnp.concatenate([shown(o < j, 128) for o in others], axis=1)
    back = jnp.concatenate([shown(o > j, 128) for o in others], axis=1)

    def fix_front(s, r):
        return jnp.concatenate([s[:, :128] + causal, s[:, 128:] + front], axis=1)

    def fix_back(s, r):
        return jnp.concatenate([s[:, :512], s[:, 512:640] + causal, s[:, 640:] + back], axis=1)

    firsts = [x_ref[256:384, :], xc_ref[256:384, :], y_ref[0:128, :], yc_ref[0:128, :]]
    seconds = [x_ref[384:512, :], xc_ref[384:512, :], y_ref[128:256, :], yc_ref[128:256, :]]
    update(qs_ref, 0, sp_ref, 896, 128, firsts, fix_front)
    update(qs_ref, 896, sp_ref, 896, 128, firsts + seconds, fix_back)

    tokens = lax.broadcasted_iota(jnp.int32, (448, 128), 0) % 64
    slots = lax.broadcasted_iota(jnp.int32, (448, 128), 1)
    mine = jnp.where(
        slots < 64,
        jnp.where(tokens >= slots, 0.0, NEG).astype(F32),
        jnp.full((448, 128), jnp.where(c == 1, 0.0, NEG), F32),
    )
    mate = shown(y == 0, 128)

    def fix_ext(s, r):
        tail = s[:, 512:] + (mine if r == 0 else mate)
        return jnp.concatenate([s[:, :512], tail], axis=1)

    update(
        qx_ref, 0, se_ref, 896, 448,
        [x_ref[0:256, :], xc_ref[0:256, :], x_ref[512:576, :], xc_ref[512:576, :]], fix_ext,
    )
    ext_planes(z, minus, plus, qx_ref, se_ref, kv_ref, [(a_ref, ac_ref), (b_ref, bc_ref)])
    token_ref[...] = jnp.zeros((8, 128), F32)
    wait()


def selected(z, planes, qs_ref, sp_ref, kv_ref, parts):
    for i, (plane, blocks) in enumerate(zip(planes, parts)):
        for side in range(2):
            @pl.when((plane > z) == (side == 1))
            def _(i=i, side=side, blocks=blocks):
                for n, block in enumerate(blocks):
                    ref, row = block[side]
                    kv_ref[i, n * 128:(n + 1) * 128, :] = ref[row:row + 128, :]

    def one(i, carry):
        plane = planes[0] if len(planes) == 1 else jnp.where(i == 0, planes[0], planes[1])
        q0 = pl.multiple_of(jnp.where(plane > z, 896, 0), 128)
        update(qs_ref, q0, sp_ref, 896, 128, [kv_ref[i, 0:512, :]])
        return carry

    if len(planes) == 1:
        one(0, 0)
    else:
        lax.fori_loop(0, 2, one, 0)


def around(idx_ref, k):
    z, _, _ = position(idx_ref)
    return z, (z + 8 - k) % 8, (z + k) % 8


def prompt_planes(idx_ref, k, now, before, y_rows, qs_ref, sp_in, sp_ref, kv_ref):
    z, minus, plus = around(idx_ref, k - 1)
    sp_ref[0:896, :] = sp_in[0:896, :]
    parts = []
    for i in range(2):
        shards = [(before[2 * i], 256), (before[2 * i + 1], 256), (now[2 * i], y_rows[i]), (now[2 * i + 1], y_rows[i])]
        parts.append([((ref, row), (ref, row + 128)) for ref, row in shards])
    fronts = [ref[row:row + 128, :] for plane in parts for (ref, row), _ in plane]
    update(qs_ref, 896, sp_ref, 896, 128, fronts, source=sp_in)
    selected(z, (minus, plus), qs_ref, sp_ref, kv_ref, parts)


def step_items(idx_ref, k, now, y_rows):
    _, minus, plus = around(idx_ref, k)
    _, minus1, plus1 = around(idx_ref, k - 1)
    am, bm = shard_at(idx_ref, minus), shard_at(idx_ref, plus)
    am1, bm1 = shard_at(idx_ref, minus1) ^ 2, shard_at(idx_ref, plus1) ^ 2
    fa, fac, fb, fbc = now
    if k < 4:
        items = [
            (am, fa, 256, 384, 512), (am ^ 1, fac, 256, 384, 512),
            (bm, fb, 256, 384, 512), (bm ^ 1, fbc, 256, 384, 512),
        ]
    else:
        items = [(am, fa, 0, 128, 256), (am ^ 1, fac, 0, 128, 256)]
    ya, yb = y_rows
    return items + [
        (am1, fa, ya, ya + 128, ya + 256), (am1 ^ 1, fac, ya, ya + 128, ya + 256),
        (bm1, fb, yb, yb + 128, yb + 256), (bm1 ^ 1, fbc, yb, yb + 128, yb + 256),
    ]


def step_body(k, *refs):
    idx_ref, table_ref, qs_ref, qx_ref = refs[:4]
    now, before = refs[4:8], refs[8:12]
    sp_in, se_in, _, sp_ref, se_ref, out_ref, token_ref, kv_ref, sems = refs[12:]
    y_rows = (576, 576)
    wait = page_copies(idx_ref, table_ref, out_ref, sems, step_items(idx_ref, k, now, y_rows))
    z, minus, plus = around(idx_ref, k)
    se_ref[...] = se_in[...]
    ext_planes(z, minus, plus, qx_ref, se_ref, kv_ref, [now[0:2], now[2:4]])
    prompt_planes(idx_ref, k, now, before, y_rows, qs_ref, sp_in, sp_ref, kv_ref)
    token_ref[...] = jnp.zeros((8, 128), F32)
    wait()


def ext_last_body(idx_ref, qx_ref, fa, fac, fb, fbc, se_in, se_ref, send_ref, kv_ref):
    z, _, plus = around(idx_ref, 4)
    se_ref[...] = se_in[...]
    kv_ref[0, 0:256, :] = fb[0:256, :]
    kv_ref[0, 256:512, :] = fbc[0:256, :]
    kv_ref[0, 512:576, :] = fa[256:320, :]
    kv_ref[0, 576:640, :] = fac[256:320, :]
    ext_plane(z, plus, qx_ref, se_ref, kv_ref.at[0])
    part = se_ref[448:896, :]
    total = part[:, HD:2 * HD]
    level = part[:, :HD] * C1 + jnp.log2(total)
    hi = level.astype(BF)
    rest = level - hi.astype(F32)
    mid = rest.astype(BF)
    low = (rest - mid.astype(F32)).astype(BF)
    lane = lax.broadcasted_iota(jnp.int32, (448, HD), 1)
    stats = jnp.where(
        lane == 0, hi.astype(F32), jnp.where(lane == 1, mid.astype(F32), low.astype(F32))
    )
    send_ref[:, :HD] = (part[:, 2 * HD:] / total).astype(BF)
    send_ref[:, HD:] = stats.astype(BF)


def prompt4_body(idx_ref, table_ref, qs_ref, *refs):
    now, before = refs[:4], refs[4:8]
    sp_in, _, sp_ref, out_ref, kv_ref, sems = refs[8:]
    y_rows = (320, 256)
    wait = page_copies(idx_ref, table_ref, out_ref, sems, step_items(idx_ref, 4, now, y_rows))
    prompt_planes(idx_ref, 4, now, before, y_rows, qs_ref, sp_in, sp_ref, kv_ref)
    wait()


def last_body(
    idx_ref, table_ref, qs_ref, g_ref, gc_ref, ra_ref, rac_ref, rb_ref, rbc_ref, sp_in, se_ref, got_ref, _,
    out_ref, pool_ref, sp_ref, kv_ref, sems,
):
    z, _, _ = position(idx_ref)
    plane = (z + 4) % 8
    shard = shard_at(idx_ref, plane) ^ 2
    wait = page_copies(
        idx_ref, table_ref, pool_ref, sems,
        [
            (shard, ra_ref, 0, None, None), (shard ^ 1, rac_ref, 0, None, None),
            (shard, rb_ref, None, 0, 128), (shard ^ 1, rbc_ref, None, 0, 128),
        ],
    )
    firsts = [g_ref[0:128, :], gc_ref[0:128, :], ra_ref[...], rac_ref[...]]
    sp_ref[0:896, :] = sp_in[0:896, :]
    update(qs_ref, 896, sp_ref, 896, 128, firsts, source=sp_in)
    blocks = [
        ((g_ref, 0), (g_ref, 128)), ((gc_ref, 0), (gc_ref, 128)), ((ra_ref, 0), (rb_ref, 0)), ((rac_ref, 0), (rbc_ref, 0))
    ]
    selected(z, (plane,), qs_ref, sp_ref, kv_ref, [blocks])

    for b in range(2):
        for h in range(HEADS):
            at = slice(b * 896 + h * 128, b * 896 + (h + 1) * 128)
            out_ref[b * 128:(b + 1) * 128, h * HD:(h + 1) * HD] = (
                sp_ref[at, 2 * HD:] / sp_ref[at, HD:2 * HD]
            ).astype(BF)
    for h in range(HEADS):
        at = slice(h * 64, (h + 1) * 64)
        total = se_ref[at, HD:2 * HD]
        level = se_ref[at, :HD] * C1 + jnp.log2(total)
        mine = se_ref[at, 2 * HD:] / total
        got = got_ref[at, :].astype(F32)
        level_y = got[:, HD:HD + 1] + got[:, HD + 1:HD + 2] + got[:, HD + 2:HD + 3]
        top = jnp.maximum(level, level_y)
        wa = jnp.exp2(level - top)
        wb = jnp.exp2(level_y - top)
        out_ref[256:320, h * HD:(h + 1) * HD] = (
            (wa * mine + wb * got[:, :HD]) / (wa + wb)
        ).astype(BF)
    wait()


def body(q_prompt, kv_prompt, q_ext, kv_ext, pool, page_slot_table):
    idx = lax.axis_index("ctx").astype(jnp.int32).reshape(1)
    kvp = kv_prompt.reshape(256, 256)
    kve = kv_ext.reshape(64, 256)
    pages = pool.reshape(6, 128, 256)

    def shift(x, d):
        return lax.ppermute(x, "ctx", [(i, (i + 4 * d) % 32) for i in range(32)])

    def flip_y(x):
        return lax.ppermute(x, "ctx", [(i, i ^ 2) for i in range(32)])

    def flip_c(x):
        return lax.ppermute(x, "ctx", [(i, i ^ 1) for i in range(32)])

    def after(x, token):
        return lax.optimization_barrier((x, token))[0]

    def arr(shape, dtype=BF):
        return jax.ShapeDtypeStruct(shape, dtype)

    def hbm(x):
        return pltpu.with_memory_space_constraint(x, pltpu.HBM)

    x, p = pl.pallas_call(
        prep_body,
        out_shape=(arr((576, 256)), arr((576, 256))),
        in_specs=[SMEM, SMEM, HBM, HBM, HBM, HBM],
        out_specs=(ANY, ANY),
        scratch_shapes=[pltpu.SemaphoreType.DMA((13,))],
        compiler_params=params(),
        name="prep",
    )(idx, page_slot_table, hbm(pages), hbm(kvp), hbm(kve), hbm(q_ext))

    yp = flip_y(p)
    a1, b1 = shift(x, 1), shift(x, -1)
    xc, yc = flip_c(x), flip_c(yp)
    n1 = (a1, flip_c(a1), b1, flip_c(b1))
    a2 = shift(jnp.concatenate([a1, yp[:320]], axis=0), 1)
    b2 = shift(jnp.concatenate([b1, yp[:320]], axis=0), -1)

    sp_t, se_t, pool_t = arr((1792, 384), F32), arr((896, 384), F32), arr((6, 128, 256))
    token_t = arr((8, 128), F32)
    sems = pltpu.SemaphoreType.DMA((25,))
    kv_t = pltpu.VMEM((2, 640, 256), BF)
    qs, qx, sp, se, new_pool, token = pl.pallas_call(
        first_body,
        out_shape=(arr((1792, 128)), arr((896, 128)), sp_t, se_t, pool_t, token_t),
        in_specs=[SMEM, SMEM] + [VMEM] * 11,
        out_specs=(VMEM,) * 4 + (HBM, VMEM),
        scratch_shapes=[kv_t, sems],
        compiler_params=params(),
        cost_estimate=cost(2e9, 3e6, 4e6),
        name="step1",
    )(idx, page_slot_table, q_prompt, q_ext, x, xc, yp, yc, *n1, pages)

    def step(k, now, before, sp, se, new_pool):
        return pl.pallas_call(
            lambda *refs: step_body(k, *refs),
            out_shape=(sp_t, se_t, pool_t, token_t),
            in_specs=[SMEM, SMEM] + [VMEM] * 12 + [HBM],
            out_specs=(VMEM, VMEM, HBM, VMEM),
            input_output_aliases={12: 0, 13: 1, 14: 2},
            scratch_shapes=[kv_t, sems],
            compiler_params=params(),
            cost_estimate=cost(2e9, 3e6, 8e6),
            name=f"step{k}",
        )(idx, page_slot_table, qs, qx, *now, *before, sp, se, new_pool)

    a2, b2 = after(a2, token), after(b2, token)
    a3, b3 = shift(a2, 1), shift(b2, -1)
    n2 = (a2, flip_c(a2), b2, flip_c(b2))
    sp, se, new_pool, token = step(2, n2, n1, sp, se, new_pool)
    a3, b3 = after(a3, token), after(b3, token)
    a4 = shift(a3[256:896], 1)
    b4 = shift(jnp.concatenate([b3[0:256], b3[576:896]], axis=0), -1)
    n3 = (a3, flip_c(a3), b3, flip_c(b3))
    sp, se, new_pool, token = step(3, n3, n2, sp, se, new_pool)
    a4, b4 = after(a4, token), after(b4, token)
    a5 = shift(a4[320:448], 1)
    b5 = shift(b4[384:576], -1)
    n4 = (a4, flip_c(a4), b4, flip_c(b4))
    se, send = pl.pallas_call(
        ext_last_body,
        out_shape=(se_t, arr((448, 256))),
        in_specs=[SMEM] + [VMEM] * 6,
        out_specs=(VMEM, VMEM),
        input_output_aliases={6: 0},
        scratch_shapes=[kv_t],
        compiler_params=params(),
        cost_estimate=cost(3e8, 6e5, 3e6),
        name="ext4",
    )(idx, qx, *n4, se)
    got = flip_y(send)
    sp, new_pool = pl.pallas_call(
        prompt4_body,
        out_shape=(sp_t, pool_t),
        in_specs=[SMEM, SMEM] + [VMEM] * 10 + [HBM],
        out_specs=(VMEM, HBM),
        input_output_aliases={11: 0, 12: 1},
        scratch_shapes=[kv_t, sems],
        compiler_params=params(),
        cost_estimate=cost(2e9, 2e6, 6e6),
        name="prompt4",
    )(idx, page_slot_table, qs, *n4, *n3, sp, new_pool)
    local_context, new_pool = pl.pallas_call(
        last_body,
        out_shape=(arr((320, 896)), pool_t),
        in_specs=[SMEM, SMEM] + [VMEM] * 10 + [HBM],
        out_specs=(VMEM, HBM),
        input_output_aliases={12: 1},
        scratch_shapes=[pltpu.VMEM((1792, 384), F32), kv_t, sems],
        compiler_params=params(),
        cost_estimate=cost(5e8, 1e6, 4e6),
        name="last",
    )(idx, page_slot_table, qs, a4, n4[1], a5, flip_c(a5), b5, flip_c(b5), sp, se, got, new_pool)
    context = lax.all_to_all(local_context, "tp", split_axis=0, concat_axis=1, tiled=True)
    return context, new_pool.reshape(6, 128, 1, 256)


def solution(mesh):
    in_specs = (
        P("ctx", "tp"),
        P("ctx", "tp", None),
        P("ctx", "tp"),
        P("ctx", "tp", None),
        P("ctx", None, "tp", None),
        P(),
    )
    out_specs = (P(("ctx", "tp"), None), P("ctx", None, "tp", None))
    return jax.shard_map(body, mesh=mesh, in_specs=in_specs, out_specs=out_specs, check_vma=False)
```

profile of v0, /device:TPU:1, one launch (start us, length us, event | category | flops | bytes accessed | tf_op | source)
XLA Modules:
  0.0 97.1 jit_solution(4144465388591075955)
XLA Ops:
  0.6 0.0 copy-start.2
  0.6 0.7 copy-done.2
  1.3 2.2 %prep.1 = (bf16[576,256]{1,0:T(8,128)(2,1)S(1)}, bf16[576,256]{1,0:T(8,128)(2,1)S(1)}) custom-call(s32[1]{0:T(128)} %bitcast.idx_ref.refs_0_, s32[144]{0:T(256)S(1)} %copy-done.2, bf16[6,128,256]{2,1,0:T(8,128)(2,1)} %bitcast.12, bf16[256,256]{1,0:T(8,128)(2,1)} %bitcast.17, bf16[64,256]{1,0:T(8,128)(2,1)} %bitcast.18, bf16[64,896]{1,0:T(8,128)(2,1)} %qe_ref.3), custom_call_target="tpu_custom_call" | custom-call | tf_op jit(solution)/shard_map/prep/pallas_call | solution.py:400
  3.6 2.2 %collective-permute-start.1 = (bf16[576,256]{1,0:T(8,128)(2,1)S(1)}, bf16[576,256]{1,0:T(8,128)(2,1)S(1)}, u32[]{:S(2)}, u32[]{:S(2)}) collective-permute-start(bf16[576,256]{1,0:T(8,128)(2,1)S(1)} %get-tuple-element.31), channel_id=1, source_target_pairs={{0,16},{8,24},{16,0},{24,8},{32,48},{40,56},{48,32},{56,40},{64,80... | collective-permute-start | bytes 884744 | tf_op jit(solution)/shard_map/ppermute | solution.py:386
  5.8 1.6 %collective-permute-start.3 = (bf16[576,256]{1,0:T(8,128)(2,1)S(1)}, bf16[576,256]{1,0:T(8,128)(2,1)S(1)}, u32[]{:S(2)}, u32[]{:S(2)}) collective-permute-start(bf16[576,256]{1,0:T(8,128)(2,1)S(1)} %get-tuple-element.30.x_ref), channel_id=1, source_target_pairs={{0,32},{8,40},{16,48},{24,56},{32,64},{40,72},{48,80},{56,88},{64,... | collective-permute-start | bytes 884744 | tf_op jit(solution)/shard_map/ppermute | solution.py:383
  7.4 3.9 %collective-permute-start.5 = (bf16[576,256]{1,0:T(8,128)(2,1)S(1)}, bf16[576,256]{1,0:T(8,128)(2,1)S(1)}, u32[]{:S(2)}, u32[]{:S(2)}) collective-permute-start(bf16[576,256]{1,0:T(8,128)(2,1)S(1)} %get-tuple-element.30.x_ref), channel_id=1, source_target_pairs={{0,224},{8,232},{16,240},{24,248},{32,0},{40,8},{48,16},{56,24},{6... | collective-permute-start | bytes 884744 | tf_op jit(solution)/shard_map/ppermute | solution.py:383
  11.3 1.2 %collective-permute-start = (bf16[576,256]{1,0:T(8,128)(2,1)S(1)}, bf16[576,256]{1,0:T(8,128)(2,1)S(1)}, u32[]{:S(2)}, u32[]{:S(2)}) collective-permute-start(bf16[576,256]{1,0:T(8,128)(2,1)S(1)} %get-tuple-element.30.x_ref), channel_id=1, source_target_pairs={{0,8},{8,0},{16,24},{24,16},{32,40},{40,32},{48,56},{56,48},{64,72... | collective-permute-start | bytes 884744 | tf_op jit(solution)/shard_map/ppermute | solution.py:389
  12.6 0.0 collective-permute-done.1.y_ref
  12.6 1.1 %collective-permute-start.2 = (bf16[576,256]{1,0:T(8,128)(2,1)S(1)}, bf16[576,256]{1,0:T(8,128)(2,1)S(1)}, u32[]{:S(2)}, u32[]{:S(2)}) collective-permute-start(bf16[576,256]{1,0:T(8,128)(2,1)S(1)} %collective-permute-done.1.y_ref), channel_id=1, source_target_pairs={{0,8},{8,0},{16,24},{24,16},{32,40},{40,32},{48,56},{56,48},{64,72... | collective-permute-start | bytes 884744 | tf_op jit(solution)/shard_map/ppermute | solution.py:389
  13.7 4.0 %collective-permute-done.3.a_ref.refs_8_ = bf16[576,256]{1,0:T(8,128)(2,1)S(1)} collective-permute-done((bf16[576,256]{1,0:T(8,128)(2,1)S(1)}, bf16[576,256]{1,0:T(8,128)(2,1)S(1)}, u32[]{:S(2)}, u32[]{:S(2)}) %collective-permute-start.3) | collective-permute-done | bytes 294944 | tf_op jit(solution)/shard_map/ppermute | solution.py:383
  17.8 1.5 %collective-permute-start.4 = (bf16[576,256]{1,0:T(8,128)(2,1)S(1)}, bf16[576,256]{1,0:T(8,128)(2,1)S(1)}, u32[]{:S(2)}, u32[]{:S(2)}) collective-permute-start(bf16[576,256]{1,0:T(8,128)(2,1)S(1)} %collective-permute-done.3.a_ref.refs_8_), channel_id=1, source_target_pairs={{0,8},{8,0},{16,24},{24,16},{32,40},{40,32},{48,56},{56,48},{64,72... | collective-permute-start | bytes 884744 | tf_op jit(solution)/shard_map/ppermute | solution.py:389
  19.3 0.0 collective-permute-done.5.b_ref.refs_10_
  19.3 0.0 collective-permute-start.6
  19.3 0.1 pad_maximum_fusion
  19.4 2.7 %collective-permute-start.10 = (bf16[896,256]{1,0:T(8,128)(2,1)S(1)}, bf16[896,256]{1,0:T(8,128)(2,1)S(1)}, u32[]{:S(2)}, u32[]{:S(2)}) collective-permute-start(bf16[896,256]{1,0:T(8,128)(2,1)S(1)} %get-tuple-element.60), channel_id=1, source_target_pairs={{0,224},{8,232},{16,240},{24,248},{32,0},{40,8},{48,16},{56,24},{6... | collective-permute-start | bytes 1376264 | tf_op jit(solution)/shard_map/ppermute | solution.py:383
  22.2 0.0 collective-permute-done.xc_ref
  22.2 0.0 collective-permute-start.7
  22.2 0.0 collective-permute-done.4.ac_ref.refs_9_
  22.2 0.0 collective-permute-done.6.bc_ref.refs_11_
  22.2 0.0 collective-permute-done.2.yc_ref
  22.2 0.0 copy-start
  22.2 1.0 %copy-done = bf16[6,128,1,256]{3,1,2,0:T(8,128)(2,1)S(1)} copy-done((bf16[6,128,1,256]{3,1,2,0:T(8,128)(2,1)S(1)}, bf16[6,128,1,256]{3,1,2,0:T(8,128)(2,1)}, u32[]{:S(2)}) %copy-start) | copy-done | bytes 393240
  23.2 0.9 copy-done.1
  24.1 1.0 %copy-done.3 = bf16[256,896]{1,0:T(8,128)(2,1)S(1)} copy-done((bf16[256,896]{1,0:T(8,128)(2,1)S(1)}, bf16[256,896]{1,0:T(8,128)(2,1)}, u32[]{:S(2)}) %copy-start.3) | copy-done | bytes 458776
  25.1 8.1 %step1.1 = (bf16[1792,128]{1,0:T(8,128)(2,1)S(1)}, bf16[896,128]{1,0:T(8,128)(2,1)S(1)}, f32[1792,384]{1,0:T(8,128)S(1)}, f32[896,384]{1,0:T(8,128)S(1)}, bf16[6...) custom-call(s32[1]{0:T(128)} %bitcast.idx_ref.refs_0_, s32[144]{0:T(256)S(1)} %copy-done.2, bf16[256,896]{1,0:T(8,128)(2,1)S(1)} %copy-done.3, ...), custom_call_target="tpu_custom_call" | custom-call | flops 2000000000 | bytes 4000000 | tf_op jit(solution)/shard_map/step1/pallas_call | solution.py:421
  33.2 0.0 collective-permute-done.10.refs_6_.refs_10_
  33.2 0.4 collective-permute-start.11
  33.6 1.6 %collective-permute-done.7.refs_4_.refs_8_ = bf16[896,256]{1,0:T(8,128)(2,1)S(1)} collective-permute-done((bf16[896,256]{1,0:T(8,128)(2,1)S(1)}, bf16[896,256]{1,0:T(8,128)(2,1)S(1)}, u32[]{:S(2)}, u32[]{:S(2)}) %collective-permute-start.7) | collective-permute-done | bytes 458784 | tf_op jit(solution)/shard_map/ppermute | solution.py:383
  35.2 1.1 %collective-permute-start.9 = (bf16[896,256]{1,0:T(8,128)(2,1)S(1)}, bf16[896,256]{1,0:T(8,128)(2,1)S(1)}, u32[]{:S(2)}, u32[]{:S(2)}) collective-permute-start(bf16[896,256]{1,0:T(8,128)(2,1)S(1)} %collective-permute-done.7.refs_4_.refs_8_), channel_id=1, source_target_pairs={{0,8},{8,0},{16,24},{24,16},{32,40},{40,32},{48,56},{56,48},{64,72... | collective-permute-start | bytes 1376264 | tf_op jit(solution)/shard_map/ppermute | solution.py:389
  36.3 0.3 collective-permute-start.14
  36.6 1.1 %collective-permute-start.8 = (bf16[896,256]{1,0:T(8,128)(2,1)S(1)}, bf16[896,256]{1,0:T(8,128)(2,1)S(1)}, u32[]{:S(2)}, u32[]{:S(2)}) collective-permute-start(bf16[896,256]{1,0:T(8,128)(2,1)S(1)} %collective-permute-done.7.refs_4_.refs_8_), channel_id=1, source_target_pairs={{0,32},{8,40},{16,48},{24,56},{32,64},{40,72},{48,80},{56,88},{64,... | collective-permute-start | bytes 1376264 | tf_op jit(solution)/shard_map/ppermute | solution.py:383
  37.8 0.0 collective-permute-done.11.refs_7_.refs_11_
  37.8 0.0 collective-permute-done.9.refs_5_.refs_9_
  37.8 8.2 %step2.1 = (f32[1792,384]{1,0:T(8,128)S(1)}, f32[896,384]{1,0:T(8,128)S(1)}, bf16[6,128,256]{2,1,0:T(8,128)(2,1)}, f32[8,128]{1,0:T(8,128)}) custom-call(s32[1]{0:T(128)} %bitcast.idx_ref.refs_0_, s32[144]{0:T(256)S(1)} %copy-done.2, ...), custom_call_target="tpu_custom_call", output_to_operand_aliasing={{0}: (12, {}), {1}: (13, {}), {2}: (14, {})} | custom-call | flops 2000000000 | bytes 8000000 | tf_op jit(solution)/shard_map/step2/pallas_call | solution.py:433
  46.0 2.4 %collective-permute-done.14.refs_6_ = bf16[896,256]{1,0:T(8,128)(2,1)S(1)} collective-permute-done((bf16[896,256]{1,0:T(8,128)(2,1)S(1)}, bf16[896,256]{1,0:T(8,128)(2,1)S(1)}, u32[]{:S(2)}, u32[]{:S(2)}) %collective-permute-start.14) | collective-permute-done | bytes 458784 | tf_op jit(solution)/shard_map/ppermute | solution.py:383
  48.5 0.8 collective-permute-start.15
  49.2 0.0 collective-permute-done.8.refs_4_
  49.2 1.5 %collective-permute-start.13 = (bf16[896,256]{1,0:T(8,128)(2,1)S(1)}, bf16[896,256]{1,0:T(8,128)(2,1)S(1)}, u32[]{:S(2)}, u32[]{:S(2)}) collective-permute-start(bf16[896,256]{1,0:T(8,128)(2,1)S(1)} %collective-permute-done.8.refs_4_), channel_id=1, source_target_pairs={{0,8},{8,0},{16,24},{24,16},{32,40},{40,32},{48,56},{56,48},{64,72... | collective-permute-start | bytes 1376264 | tf_op jit(solution)/shard_map/ppermute | solution.py:389
  50.9 0.1 collective-permute-start.12
  51.0 2.7 %collective-permute-start.19 = (bf16[576,256]{1,0:T(8,128)(2,1)S(1)}, bf16[576,256]{1,0:T(8,128)(2,1)S(1)}, u32[]{:S(2)}, u32[]{:S(2)}) collective-permute-start(bf16[576,256]{1,0:T(8,128)(2,1)S(1)} %pad_maximum_fusion.2), channel_id=1, source_target_pairs={{0,224},{8,232},{16,240},{24,248},{32,0},{40,8},{48,16},{56,24},{6... | collective-permute-start | bytes 884744 | tf_op jit(solution)/shard_map/ppermute | solution.py:383
  53.7 0.0 collective-permute-done.15.refs_7_
  53.7 0.0 collective-permute-done.13.refs_5_
  53.7 8.2 %step3.1 = (f32[1792,384]{1,0:T(8,128)S(1)}, f32[896,384]{1,0:T(8,128)S(1)}, bf16[6,128,256]{2,1,0:T(8,128)(2,1)}, f32[8,128]{1,0:T(8,128)}) custom-call(s32[1]{0:T(128)} %bitcast.idx_ref.refs_0_, s32[144]{0:T(256)S(1)} %copy-done.2, ...), custom_call_target="tpu_custom_call", output_to_operand_aliasing={{0}: (12, {}), {1}: (13, {}), {2}: (14, {})} | custom-call | flops 2000000000 | bytes 8000000 | tf_op jit(solution)/shard_map/step3/pallas_call | solution.py:433
  62.0 0.0 collective-permute-done.12.refs_0_.fa.g_ref
  62.0 0.9 collective-permute-start.16
  62.8 0.0 collective-permute-done.19.refs_2_.fb
  62.8 0.1 collective-permute-start.22
  63.0 1.5 %collective-permute-start.20 = (bf16[192,256]{1,0:T(8,128)(2,1)S(1)}, bf16[192,256]{1,0:T(8,128)(2,1)S(1)}, u32[]{:S(2)}, u32[]{:S(2)}) collective-permute-start(bf16[192,256]{1,0:T(8,128)(2,1)S(1)} %slice.24), channel_id=1, source_target_pairs={{0,224},{8,232},{16,240},{24,248},{32,0},{40,8},{48,16},{56,24},{6... | collective-permute-start | bytes 294920 | tf_op jit(solution)/shard_map/ppermute | solution.py:383
  64.4 0.1 collective-permute-start.17
  64.5 0.0 collective-permute-done.22.refs_3_.fbc
  64.5 0.0 collective-permute-done.16.refs_1_.fac.gc_ref
  64.5 1.3 %ext4.1 = (f32[896,384]{1,0:T(8,128)S(1)}, bf16[448,256]{1,0:T(8,128)(2,1)S(1)}) custom-call(s32[1]{0:T(128)} %bitcast.idx_ref.refs_0_, bf16[896,128]{1,0:T(8,128)(2,1)S(1)} %get-tuple-element.35.refs_3_.qx_ref, bf16[640,256]{1,0:T(8,128)(2,1)S(1)} %collective-permute-done.12.refs_0_.fa.g_ref, ...), custom_call_target="tpu_custom_call", output_to_operand_aliasing={{0}: (6, {})} | custom-call | flops 300000000 | bytes 3000000 | tf_op jit(solution)/shard_map/ext4/pallas_call | solution.py:458
  65.9 0.3 collective-permute-start.23
  66.1 2.6 %collective-permute-done.17.ra_ref = bf16[128,256]{1,0:T(8,128)(2,1)S(1)} collective-permute-done((bf16[128,256]{1,0:T(8,128)(2,1)S(1)}, bf16[128,256]{1,0:T(8,128)(2,1)S(1)}, u32[]{:S(2)}, u32[]{:S(2)}) %collective-permute-start.17) | collective-permute-done | bytes 65568 | tf_op jit(solution)/shard_map/ppermute | solution.py:383
  68.8 1.4 %collective-permute-start.18 = (bf16[128,256]{1,0:T(8,128)(2,1)S(1)}, bf16[128,256]{1,0:T(8,128)(2,1)S(1)}, u32[]{:S(2)}, u32[]{:S(2)}) collective-permute-start(bf16[128,256]{1,0:T(8,128)(2,1)S(1)} %collective-permute-done.17.ra_ref), channel_id=1, source_target_pairs={{0,8},{8,0},{16,24},{24,16},{32,40},{40,32},{48,56},{56,48},{64,72... | collective-permute-start | bytes 196616 | tf_op jit(solution)/shard_map/ppermute | solution.py:389
  70.2 0.0 collective-permute-done.20.rb_ref
  70.2 0.0 collective-permute-start.21
  70.2 4.9 %prompt4.1 = (f32[1792,384]{1,0:T(8,128)S(1)}, bf16[6,128,256]{2,1,0:T(8,128)(2,1)}) custom-call(s32[1]{0:T(128)} %bitcast.idx_ref.refs_0_, s32[144]{0:T(256)S(1)} %copy-done.2, bf16[1792,128]{1,0:T(8,128)(2,1)S(1)} %get-tuple-element.32.refs_2_.qs_ref, ...), custom_call_target="tpu_custom_call", output_to_operand_aliasing={{0}: (11, {}), {1}: (12, {})} | custom-call | flops 2000000000 | bytes 6000000 | tf_op jit(solution)/shard_map/prompt4/pallas_call | solution.py:470
  75.2 0.0 collective-permute-done.18.rac_ref
  75.2 0.0 collective-permute-done.21.rbc_ref
  75.2 0.0 collective-permute-done.23.got_ref
  75.2 3.6 %last.1 = (bf16[320,896]{1,0:T(8,128)(2,1)S(1)}, bf16[6,128,256]{2,1,0:T(8,128)(2,1)}) custom-call(s32[1]{0:T(128)} %bitcast.idx_ref.refs_0_, s32[144]{0:T(256)S(1)} %copy-done.2, bf16[1792,128]{1,0:T(8,128)(2,1)S(1)} %get-tuple-element.32.refs_2_.qs_ref, ...), custom_call_target="tpu_custom_call", output_to_operand_aliasing={{1}: (12, {})} | custom-call | flops 500000000 | bytes 4000000 | tf_op jit(solution)/shard_map/last/pallas_call | solution.py:481
  78.8 17.4 %all_to_all.19 = bf16[8,40,896]{2,1,0:T(8,128)(2,1)S(1)} all-to-all(bf16[8,40,896]{2,1,0:T(8,128)(2,1)S(1)} %bitcast.11), channel_id=1, replica_groups=mesh['ctx'=32,'tp'=8] {'tp'}, dimensions={0} | all-to-all | bytes 1146880 | tf_op jit(solution)/shard_map/all_to_all | solution.py:492
  96.2 0.9 copy.20
  (9 shorter events, 0.1 us)
Async XLA Ops:
  0.6 0.7 copy-start.2
  3.6 9.0 %collective-permute-start.1 = (bf16[576,256]{1,0:T(8,128)(2,1)S(1)}, bf16[576,256]{1,0:T(8,128)(2,1)S(1)}, u32[]{:S(2)}, u32[]{:S(2)}) collective-permute-start(bf16[576,256]{1,0:T(8,128)(2,1)S(1)} %get-tuple-element.31), channel_id=1, source_target_pairs={{0,16},{8,24},{16,0},{24,8},{32,48},{40,56},{48,32},{56,40},{64,80... | collective-permute-start | bytes 884744 | tf_op jit(solution)/shard_map/ppermute | solution.py:386
  5.8 12.0 %collective-permute-start.3 = (bf16[576,256]{1,0:T(8,128)(2,1)S(1)}, bf16[576,256]{1,0:T(8,128)(2,1)S(1)}, u32[]{:S(2)}, u32[]{:S(2)}) collective-permute-start(bf16[576,256]{1,0:T(8,128)(2,1)S(1)} %get-tuple-element.30.x_ref), channel_id=1, source_target_pairs={{0,32},{8,40},{16,48},{24,56},{32,64},{40,72},{48,80},{56,88},{64,... | collective-permute-start | bytes 884744 | tf_op jit(solution)/shard_map/ppermute | solution.py:383
  7.4 11.9 %collective-permute-start.5 = (bf16[576,256]{1,0:T(8,128)(2,1)S(1)}, bf16[576,256]{1,0:T(8,128)(2,1)S(1)}, u32[]{:S(2)}, u32[]{:S(2)}) collective-permute-start(bf16[576,256]{1,0:T(8,128)(2,1)S(1)} %get-tuple-element.30.x_ref), channel_id=1, source_target_pairs={{0,224},{8,232},{16,240},{24,248},{32,0},{40,8},{48,16},{56,24},{6... | collective-permute-start | bytes 884744 | tf_op jit(solution)/shard_map/ppermute | solution.py:383
  11.3 10.8 %collective-permute-start = (bf16[576,256]{1,0:T(8,128)(2,1)S(1)}, bf16[576,256]{1,0:T(8,128)(2,1)S(1)}, u32[]{:S(2)}, u32[]{:S(2)}) collective-permute-start(bf16[576,256]{1,0:T(8,128)(2,1)S(1)} %get-tuple-element.30.x_ref), channel_id=1, source_target_pairs={{0,8},{8,0},{16,24},{24,16},{32,40},{40,32},{48,56},{56,48},{64,72... | collective-permute-start | bytes 884744 | tf_op jit(solution)/shard_map/ppermute | solution.py:389
  12.6 9.6 %collective-permute-start.2 = (bf16[576,256]{1,0:T(8,128)(2,1)S(1)}, bf16[576,256]{1,0:T(8,128)(2,1)S(1)}, u32[]{:S(2)}, u32[]{:S(2)}) collective-permute-start(bf16[576,256]{1,0:T(8,128)(2,1)S(1)} %collective-permute-done.1.y_ref), channel_id=1, source_target_pairs={{0,8},{8,0},{16,24},{24,16},{32,40},{40,32},{48,56},{56,48},{64,72... | collective-permute-start | bytes 884744 | tf_op jit(solution)/shard_map/ppermute | solution.py:389
  17.8 4.4 %collective-permute-start.4 = (bf16[576,256]{1,0:T(8,128)(2,1)S(1)}, bf16[576,256]{1,0:T(8,128)(2,1)S(1)}, u32[]{:S(2)}, u32[]{:S(2)}) collective-permute-start(bf16[576,256]{1,0:T(8,128)(2,1)S(1)} %collective-permute-done.3.a_ref.refs_8_), channel_id=1, source_target_pairs={{0,8},{8,0},{16,24},{24,16},{32,40},{40,32},{48,56},{56,48},{64,72... | collective-permute-start | bytes 884744 | tf_op jit(solution)/shard_map/ppermute | solution.py:389
  19.3 2.9 %collective-permute-start.6 = (bf16[576,256]{1,0:T(8,128)(2,1)S(1)}, bf16[576,256]{1,0:T(8,128)(2,1)S(1)}, u32[]{:S(2)}, u32[]{:S(2)}) collective-permute-start(bf16[576,256]{1,0:T(8,128)(2,1)S(1)} %collective-permute-done.5.b_ref.refs_10_), channel_id=1, source_target_pairs={{0,8},{8,0},{16,24},{24,16},{32,40},{40,32},{48,56},{56,48},{64,72... | collective-permute-start | bytes 884744 | tf_op jit(solution)/shard_map/ppermute | solution.py:389
  19.4 13.8 %collective-permute-start.10 = (bf16[896,256]{1,0:T(8,128)(2,1)S(1)}, bf16[896,256]{1,0:T(8,128)(2,1)S(1)}, u32[]{:S(2)}, u32[]{:S(2)}) collective-permute-start(bf16[896,256]{1,0:T(8,128)(2,1)S(1)} %get-tuple-element.60), channel_id=1, source_target_pairs={{0,224},{8,232},{16,240},{24,248},{32,0},{40,8},{48,16},{56,24},{6... | collective-permute-start | bytes 1376264 | tf_op jit(solution)/shard_map/ppermute | solution.py:383
  22.2 13.0 %collective-permute-start.7 = (bf16[896,256]{1,0:T(8,128)(2,1)S(1)}, bf16[896,256]{1,0:T(8,128)(2,1)S(1)}, u32[]{:S(2)}, u32[]{:S(2)}) collective-permute-start(bf16[896,256]{1,0:T(8,128)(2,1)S(1)} %get-tuple-element.61), channel_id=1, source_target_pairs={{0,32},{8,40},{16,48},{24,56},{32,64},{40,72},{48,80},{56,88},{64,... | collective-permute-start | bytes 1376264 | tf_op jit(solution)/shard_map/ppermute | solution.py:383
  22.2 1.0 %copy-start = (bf16[6,128,1,256]{3,1,2,0:T(8,128)(2,1)S(1)}, bf16[6,128,1,256]{3,1,2,0:T(8,128)(2,1)}, u32[]{:S(2)}) copy-start(bf16[6,128,1,256]{3,1,2,0:T(8,128)(2,1)} %param.10) | copy-start | bytes 1179652
  23.2 0.9 copy-start.1
  24.1 1.0 %copy-start.3 = (bf16[256,896]{1,0:T(8,128)(2,1)S(1)}, bf16[256,896]{1,0:T(8,128)(2,1)}, u32[]{:S(2)}) copy-start(bf16[256,896]{1,0:T(8,128)(2,1)} %qp_ref.1) | copy-start | bytes 1376260
  33.2 4.6 %collective-permute-start.11 = (bf16[896,256]{1,0:T(8,128)(2,1)S(1)}, bf16[896,256]{1,0:T(8,128)(2,1)S(1)}, u32[]{:S(2)}, u32[]{:S(2)}) collective-permute-start(bf16[896,256]{1,0:T(8,128)(2,1)S(1)} %collective-permute-done.10.refs_6_.refs_10_), channel_id=1, source_target_pairs={{0,8},{8,0},{16,24},{24,16},{32,40},{40,32},{48,56},{56,48},{64,72... | collective-permute-start | bytes 1376264 | tf_op jit(solution)/shard_map/ppermute | solution.py:389
  35.2 2.6 %collective-permute-start.9 = (bf16[896,256]{1,0:T(8,128)(2,1)S(1)}, bf16[896,256]{1,0:T(8,128)(2,1)S(1)}, u32[]{:S(2)}, u32[]{:S(2)}) collective-permute-start(bf16[896,256]{1,0:T(8,128)(2,1)S(1)} %collective-permute-done.7.refs_4_.refs_8_), channel_id=1, source_target_pairs={{0,8},{8,0},{16,24},{24,16},{32,40},{40,32},{48,56},{56,48},{64,72... | collective-permute-start | bytes 1376264 | tf_op jit(solution)/shard_map/ppermute | solution.py:389
  36.3 12.2 %collective-permute-start.14 = (bf16[896,256]{1,0:T(8,128)(2,1)S(1)}, bf16[896,256]{1,0:T(8,128)(2,1)S(1)}, u32[]{:S(2)}, u32[]{:S(2)}) collective-permute-start(bf16[896,256]{1,0:T(8,128)(2,1)S(1)} %collective-permute-done.10.refs_6_.refs_10_), channel_id=1, source_target_pairs={{0,224},{8,232},{16,240},{24,248},{32,0},{40,8},{48,16},{56,24},{6... | collective-permute-start | bytes 1376264 | tf_op jit(solution)/shard_map/ppermute | solution.py:383
  36.6 12.6 %collective-permute-start.8 = (bf16[896,256]{1,0:T(8,128)(2,1)S(1)}, bf16[896,256]{1,0:T(8,128)(2,1)S(1)}, u32[]{:S(2)}, u32[]{:S(2)}) collective-permute-start(bf16[896,256]{1,0:T(8,128)(2,1)S(1)} %collective-permute-done.7.refs_4_.refs_8_), channel_id=1, source_target_pairs={{0,32},{8,40},{16,48},{24,56},{32,64},{40,72},{48,80},{56,88},{64,... | collective-permute-start | bytes 1376264 | tf_op jit(solution)/shard_map/ppermute | solution.py:383
  48.5 5.2 %collective-permute-start.15 = (bf16[896,256]{1,0:T(8,128)(2,1)S(1)}, bf16[896,256]{1,0:T(8,128)(2,1)S(1)}, u32[]{:S(2)}, u32[]{:S(2)}) collective-permute-start(bf16[896,256]{1,0:T(8,128)(2,1)S(1)} %collective-permute-done.14.refs_6_), channel_id=1, source_target_pairs={{0,8},{8,0},{16,24},{24,16},{32,40},{40,32},{48,56},{56,48},{64,72... | collective-permute-start | bytes 1376264 | tf_op jit(solution)/shard_map/ppermute | solution.py:389
  49.2 4.5 %collective-permute-start.13 = (bf16[896,256]{1,0:T(8,128)(2,1)S(1)}, bf16[896,256]{1,0:T(8,128)(2,1)S(1)}, u32[]{:S(2)}, u32[]{:S(2)}) collective-permute-start(bf16[896,256]{1,0:T(8,128)(2,1)S(1)} %collective-permute-done.8.refs_4_), channel_id=1, source_target_pairs={{0,8},{8,0},{16,24},{24,16},{32,40},{40,32},{48,56},{56,48},{64,72... | collective-permute-start | bytes 1376264 | tf_op jit(solution)/shard_map/ppermute | solution.py:389
  50.9 11.1 %collective-permute-start.12 = (bf16[640,256]{1,0:T(8,128)(2,1)S(1)}, bf16[640,256]{1,0:T(8,128)(2,1)S(1)}, u32[]{:S(2)}, u32[]{:S(2)}) collective-permute-start(bf16[640,256]{1,0:T(8,128)(2,1)S(1)} %slice.20), channel_id=1, source_target_pairs={{0,32},{8,40},{16,48},{24,56},{32,64},{40,72},{48,80},{56,88},{64,... | collective-permute-start | bytes 983048 | tf_op jit(solution)/shard_map/ppermute | solution.py:383
  51.0 11.9 %collective-permute-start.19 = (bf16[576,256]{1,0:T(8,128)(2,1)S(1)}, bf16[576,256]{1,0:T(8,128)(2,1)S(1)}, u32[]{:S(2)}, u32[]{:S(2)}) collective-permute-start(bf16[576,256]{1,0:T(8,128)(2,1)S(1)} %pad_maximum_fusion.2), channel_id=1, source_target_pairs={{0,224},{8,232},{16,240},{24,248},{32,0},{40,8},{48,16},{56,24},{6... | collective-permute-start | bytes 884744 | tf_op jit(solution)/shard_map/ppermute | solution.py:383
  62.0 2.6 %collective-permute-start.16 = (bf16[640,256]{1,0:T(8,128)(2,1)S(1)}, bf16[640,256]{1,0:T(8,128)(2,1)S(1)}, u32[]{:S(2)}, u32[]{:S(2)}) collective-permute-start(bf16[640,256]{1,0:T(8,128)(2,1)S(1)} %collective-permute-done.12.refs_0_.fa.g_ref), channel_id=1, source_target_pairs={{0,8},{8,0},{16,24},{24,16},{32,40},{40,32},{48,56},{56,48},{64,72... | collective-permute-start | bytes 983048 | tf_op jit(solution)/shard_map/ppermute | solution.py:389
  62.8 1.7 %collective-permute-start.22 = (bf16[576,256]{1,0:T(8,128)(2,1)S(1)}, bf16[576,256]{1,0:T(8,128)(2,1)S(1)}, u32[]{:S(2)}, u32[]{:S(2)}) collective-permute-start(bf16[576,256]{1,0:T(8,128)(2,1)S(1)} %collective-permute-done.19.refs_2_.fb), channel_id=1, source_target_pairs={{0,8},{8,0},{16,24},{24,16},{32,40},{40,32},{48,56},{56,48},{64,72... | collective-permute-start | bytes 884744 | tf_op jit(solution)/shard_map/ppermute | solution.py:389
  63.0 7.2 %collective-permute-start.20 = (bf16[192,256]{1,0:T(8,128)(2,1)S(1)}, bf16[192,256]{1,0:T(8,128)(2,1)S(1)}, u32[]{:S(2)}, u32[]{:S(2)}) collective-permute-start(bf16[192,256]{1,0:T(8,128)(2,1)S(1)} %slice.24), channel_id=1, source_target_pairs={{0,224},{8,232},{16,240},{24,248},{32,0},{40,8},{48,16},{56,24},{6... | collective-permute-start | bytes 294920 | tf_op jit(solution)/shard_map/ppermute | solution.py:383
  64.4 4.3 %collective-permute-start.17 = (bf16[128,256]{1,0:T(8,128)(2,1)S(1)}, bf16[128,256]{1,0:T(8,128)(2,1)S(1)}, u32[]{:S(2)}, u32[]{:S(2)}) collective-permute-start(bf16[128,256]{1,0:T(8,128)(2,1)S(1)} %slice.21), channel_id=1, source_target_pairs={{0,32},{8,40},{16,48},{24,56},{32,64},{40,72},{48,80},{56,88},{64,... | collective-permute-start | bytes 196616 | tf_op jit(solution)/shard_map/ppermute | solution.py:383
  65.9 9.3 %collective-permute-start.23 = (bf16[448,256]{1,0:T(8,128)(2,1)S(1)}, bf16[448,256]{1,0:T(8,128)(2,1)S(1)}, u32[]{:S(2)}, u32[]{:S(2)}) collective-permute-start(bf16[448,256]{1,0:T(8,128)(2,1)S(1)} %get-tuple-element.54), channel_id=1, source_target_pairs={{0,16},{8,24},{16,0},{24,8},{32,48},{40,56},{48,32},{56,40},{64,80... | collective-permute-start | bytes 688136 | tf_op jit(solution)/shard_map/ppermute | solution.py:386
  68.8 6.4 %collective-permute-start.18 = (bf16[128,256]{1,0:T(8,128)(2,1)S(1)}, bf16[128,256]{1,0:T(8,128)(2,1)S(1)}, u32[]{:S(2)}, u32[]{:S(2)}) collective-permute-start(bf16[128,256]{1,0:T(8,128)(2,1)S(1)} %collective-permute-done.17.ra_ref), channel_id=1, source_target_pairs={{0,8},{8,0},{16,24},{24,16},{32,40},{40,32},{48,56},{56,48},{64,72... | collective-permute-start | bytes 196616 | tf_op jit(solution)/shard_map/ppermute | solution.py:389
  70.2 5.0 %collective-permute-start.21 = (bf16[192,256]{1,0:T(8,128)(2,1)S(1)}, bf16[192,256]{1,0:T(8,128)(2,1)S(1)}, u32[]{:S(2)}, u32[]{:S(2)}) collective-permute-start(bf16[192,256]{1,0:T(8,128)(2,1)S(1)} %collective-permute-done.20.rb_ref), channel_id=1, source_target_pairs={{0,8},{8,0},{16,24},{24,16},{32,40},{40,32},{48,56},{56,48},{64,72... | collective-permute-start | bytes 294920 | tf_op jit(solution)/shard_map/ppermute | solution.py:389
where the time goes:
time: 97.4 us; the launch traced here: 97.1 us
  Pallas kernels  36.7 us (38%)
  starting transfers between devices  26.8 us (28%)
  blocking collectives  17.4 us (18%)
  waiting for transfers between devices  10.7 us (11%)
  local copies, waits for them, and re-layouts  4.53 us (5%)
    all_to_all x1, blocking collectives, body(): lax.all_to_all(local_context, 'tp', split_axis=0, concat_axis=1, tiled=True)  17.4 us
    pallas_call x2, Pallas kernels, step(): pl.pallas_call(lambda *refs: step_body(k, *refs), out_shape=(sp_t, se_t,...  16.5 us
    ppermute x10, starting transfers between devices, shift(): return lax.ppermute(x, 'ctx', [(i, (i + 4 * d) % 32) for i in range(32)])  14.1 us
    ppermute x10, waiting for transfers between devices, shift(): return lax.ppermute(x, 'ctx', [(i, (i + 4 * d) % 32) for i in range(32)])  10.7 us
    ppermute x12, starting transfers between devices, flip_c(): return lax.ppermute(x, 'ctx', [(i, i ^ 1) for i in range(32)])  10.1 us
    pallas_call x1, Pallas kernels, body(): pl.pallas_call(first_body, out_shape=(arr((1792, 128)), arr((896, 128)),...  8.09 us
    pallas_call x1, Pallas kernels, body(): pl.pallas_call(prompt4_body, out_shape=(sp_t, pool_t), in_specs=[SMEM, SM...  4.94 us
    pallas_call x1, Pallas kernels, body(): pl.pallas_call(last_body, out_shape=(arr((320, 896)), pool_t), in_specs=[...  3.61 us
  transfers between devices with their start and end apart: 24, of which 4 were waited for; matrix products, arithmetic and copies ran while one was open for 0% of the time, Pallas kernels for 32%

commit v1 on v0

--- a/solution.py
+++ b/solution.py
@@ -75,7 +75,10 @@
         early.append(pltpu.make_async_copy(qe_ref.at[:, h * HD:(h + 1) * HD], to, sems.at[6 + h]))
     for copy in early:
         copy.start()
-    _, a, b = lax.fori_loop(0, 64, scan, (zero, zero, zero))
+    found = (zero, zero, zero)
+    for j in range(64):
+        found = scan(j, found)
+    _, a, b = found
     late = [
         pltpu.make_async_copy(pool_ref.at[a], x_ref.at[0:128], sems.at[4]),
         pltpu.make_async_copy(pool_ref.at[b], x_ref.at[128:256], sems.at[5]),
@@ -405,7 +408,7 @@
         scratch_shapes=[pltpu.SemaphoreType.DMA((13,))],
         compiler_params=params(),
         name="prep",
-    )(idx, page_slot_table, hbm(pages), hbm(kvp), hbm(kve), hbm(q_ext))
+    )(idx, hbm(page_slot_table), hbm(pages), hbm(kvp), hbm(kve), hbm(q_ext))
 
     yp = flip_y(p)
     a1, b1 = shift(x, 1), shift(x, -1)

time: 97.4 us -> 97.2 us (level)
  transfers between devices with their start and end apart: 24 -> 24, of which waited for: 4 -> 5; matrix products, arithmetic and copies ran while one was open for 0% -> 0% of each run, Pallas kernels for 32% -> 32%
where the time goes in v1:
time: 97.2 us; the launch traced here: 96.9 us
  Pallas kernels  36.7 us (38%)
  starting transfers between devices  26.6 us (27%)
  blocking collectives  17.4 us (18%)
  waiting for transfers between devices  10.7 us (11%)
  local copies, waits for them, and re-layouts  4.53 us (5%)
    all_to_all x1, blocking collectives, body(): lax.all_to_all(local_context, 'tp', split_axis=0, concat_axis=1, tiled=True)  17.4 us
    pallas_call x2, Pallas kernels, step(): pl.pallas_call(lambda *refs: step_body(k, *refs), out_shape=(sp_t, se_t,...  16.7 us
    ppermute x10, starting transfers between devices, shift(): return lax.ppermute(x, 'ctx', [(i, (i + 4 * d) % 32) for i in range(32)])  14.1 us
    ppermute x10, waiting for transfers between devices, shift(): return lax.ppermute(x, 'ctx', [(i, (i + 4 * d) % 32) for i in range(32)])  10.7 us
    ppermute x12, starting transfers between devices, flip_c(): return lax.ppermute(x, 'ctx', [(i, i ^ 1) for i in range(32)])  9.95 us
    pallas_call x1, Pallas kernels, body(): pl.pallas_call(first_body, out_shape=(arr((1792, 128)), arr((896, 128)),...  8.09 us
    pallas_call x1, Pallas kernels, body(): pl.pallas_call(prompt4_body, out_shape=(sp_t, pool_t), in_specs=[SMEM, SM...  4.95 us
    pallas_call x1, Pallas kernels, body(): pl.pallas_call(last_body, out_shape=(arr((320, 896)), pool_t), in_specs=[...  3.61 us
  transfers between devices with their start and end apart: 24, of which 5 were waited for; matrix products, arithmetic and copies ran while one was open for 0% of the time, Pallas kernels for 32%

profile of v1, /device:TPU:1, one launch (start us, length us, event | category | flops | bytes accessed | tf_op | source)
XLA Modules:
  0.0 96.9 jit_solution(5041788209408800165)
XLA Ops:
  0.6 2.0 %prep.1 = (bf16[576,256]{1,0:T(8,128)(2,1)S(1)}, bf16[576,256]{1,0:T(8,128)(2,1)S(1)}) custom-call(s32[1]{0:T(128)} %bitcast.idx_ref.refs_0_, s32[144]{0:T(256)} %table_ref.7, bf16[6,128,256]{2,1,0:T(8,128)(2,1)} %bitcast.12, bf16[256,256]{1,0:T(8,128)(2,1)} %bitcast.17, bf16[64,256]{1,0:T(8,128)(2,1)} %bitcast.18, bf16[64,896]{1,0:T(8,128)(2,1)} %qe_ref.3), custom_call_target="tpu_custom_call" | custom-call | tf_op jit(solution)/shard_map/prep/pallas_call | solution.py:403
  2.6 2.2 %collective-permute-start.1 = (bf16[576,256]{1,0:T(8,128)(2,1)S(1)}, bf16[576,256]{1,0:T(8,128)(2,1)S(1)}, u32[]{:S(2)}, u32[]{:S(2)}) collective-permute-start(bf16[576,256]{1,0:T(8,128)(2,1)S(1)} %get-tuple-element.31), channel_id=1, source_target_pairs={{0,16},{8,24},{16,0},{24,8},{32,48},{40,56},{48,32},{56,40},{64,80... | collective-permute-start | bytes 884744 | tf_op jit(solution)/shard_map/ppermute | solution.py:389
  4.8 1.6 %collective-permute-start.3 = (bf16[576,256]{1,0:T(8,128)(2,1)S(1)}, bf16[576,256]{1,0:T(8,128)(2,1)S(1)}, u32[]{:S(2)}, u32[]{:S(2)}) collective-permute-start(bf16[576,256]{1,0:T(8,128)(2,1)S(1)} %get-tuple-element.30.x_ref), channel_id=1, source_target_pairs={{0,32},{8,40},{16,48},{24,56},{32,64},{40,72},{48,80},{56,88},{64,... | collective-permute-start | bytes 884744 | tf_op jit(solution)/shard_map/ppermute | solution.py:386
  6.5 3.9 %collective-permute-start.5 = (bf16[576,256]{1,0:T(8,128)(2,1)S(1)}, bf16[576,256]{1,0:T(8,128)(2,1)S(1)}, u32[]{:S(2)}, u32[]{:S(2)}) collective-permute-start(bf16[576,256]{1,0:T(8,128)(2,1)S(1)} %get-tuple-element.30.x_ref), channel_id=1, source_target_pairs={{0,224},{8,232},{16,240},{24,248},{32,0},{40,8},{48,16},{56,24},{6... | collective-permute-start | bytes 884744 | tf_op jit(solution)/shard_map/ppermute | solution.py:386
  10.4 1.2 %collective-permute-start = (bf16[576,256]{1,0:T(8,128)(2,1)S(1)}, bf16[576,256]{1,0:T(8,128)(2,1)S(1)}, u32[]{:S(2)}, u32[]{:S(2)}) collective-permute-start(bf16[576,256]{1,0:T(8,128)(2,1)S(1)} %get-tuple-element.30.x_ref), channel_id=1, source_target_pairs={{0,8},{8,0},{16,24},{24,16},{32,40},{40,32},{48,56},{56,48},{64,72... | collective-permute-start | bytes 884744 | tf_op jit(solution)/shard_map/ppermute | solution.py:392
  11.7 0.0 collective-permute-done.1.y_ref
  11.7 1.1 %collective-permute-start.2 = (bf16[576,256]{1,0:T(8,128)(2,1)S(1)}, bf16[576,256]{1,0:T(8,128)(2,1)S(1)}, u32[]{:S(2)}, u32[]{:S(2)}) collective-permute-start(bf16[576,256]{1,0:T(8,128)(2,1)S(1)} %collective-permute-done.1.y_ref), channel_id=1, source_target_pairs={{0,8},{8,0},{16,24},{24,16},{32,40},{40,32},{48,56},{56,48},{64,72... | collective-permute-start | bytes 884744 | tf_op jit(solution)/shard_map/ppermute | solution.py:392
  12.8 4.0 %collective-permute-done.3.a_ref.refs_8_ = bf16[576,256]{1,0:T(8,128)(2,1)S(1)} collective-permute-done((bf16[576,256]{1,0:T(8,128)(2,1)S(1)}, bf16[576,256]{1,0:T(8,128)(2,1)S(1)}, u32[]{:S(2)}, u32[]{:S(2)}) %collective-permute-start.3) | collective-permute-done | bytes 294944 | tf_op jit(solution)/shard_map/ppermute | solution.py:386
  16.8 1.5 %collective-permute-start.4 = (bf16[576,256]{1,0:T(8,128)(2,1)S(1)}, bf16[576,256]{1,0:T(8,128)(2,1)S(1)}, u32[]{:S(2)}, u32[]{:S(2)}) collective-permute-start(bf16[576,256]{1,0:T(8,128)(2,1)S(1)} %collective-permute-done.3.a_ref.refs_8_), channel_id=1, source_target_pairs={{0,8},{8,0},{16,24},{24,16},{32,40},{40,32},{48,56},{56,48},{64,72... | collective-permute-start | bytes 884744 | tf_op jit(solution)/shard_map/ppermute | solution.py:392
  18.4 0.0 collective-permute-done.5.b_ref.refs_10_
  18.4 0.0 collective-permute-start.6
  18.4 0.1 pad_maximum_fusion
  18.5 2.7 %collective-permute-start.10 = (bf16[896,256]{1,0:T(8,128)(2,1)S(1)}, bf16[896,256]{1,0:T(8,128)(2,1)S(1)}, u32[]{:S(2)}, u32[]{:S(2)}) collective-permute-start(bf16[896,256]{1,0:T(8,128)(2,1)S(1)} %get-tuple-element.60), channel_id=1, source_target_pairs={{0,224},{8,232},{16,240},{24,248},{32,0},{40,8},{48,16},{56,24},{6... | collective-permute-start | bytes 1376264 | tf_op jit(solution)/shard_map/ppermute | solution.py:386
  21.2 0.0 collective-permute-done.xc_ref
  21.2 0.0 collective-permute-start.7
  21.2 0.0 collective-permute-done.4.ac_ref.refs_9_
  21.2 0.0 collective-permute-done.6.bc_ref.refs_11_
  21.3 0.0 collective-permute-done.2.yc_ref
  21.3 0.0 copy-start
  21.3 1.0 %copy-done = bf16[6,128,1,256]{3,1,2,0:T(8,128)(2,1)S(1)} copy-done((bf16[6,128,1,256]{3,1,2,0:T(8,128)(2,1)S(1)}, bf16[6,128,1,256]{3,1,2,0:T(8,128)(2,1)}, u32[]{:S(2)}) %copy-start) | copy-done | bytes 393240
  22.3 0.0 copy-start.1
  22.3 0.9 copy-done.1
  23.2 0.7 copy-done.2
  23.8 1.0 %copy-done.3 = bf16[256,896]{1,0:T(8,128)(2,1)S(1)} copy-done((bf16[256,896]{1,0:T(8,128)(2,1)S(1)}, bf16[256,896]{1,0:T(8,128)(2,1)}, u32[]{:S(2)}) %copy-start.3) | copy-done | bytes 458776
  24.9 8.1 %step1.1 = (bf16[1792,128]{1,0:T(8,128)(2,1)S(1)}, bf16[896,128]{1,0:T(8,128)(2,1)S(1)}, f32[1792,384]{1,0:T(8,128)S(1)}, f32[896,384]{1,0:T(8,128)S(1)}, bf16[6...) custom-call(s32[1]{0:T(128)} %bitcast.idx_ref.refs_0_, s32[144]{0:T(256)S(1)} %copy-done.2, bf16[256,896]{1,0:T(8,128)(2,1)S(1)} %copy-done.3, ...), custom_call_target="tpu_custom_call" | custom-call | flops 2000000000 | bytes 4000000 | tf_op jit(solution)/shard_map/step1/pallas_call | solution.py:424
  33.0 0.0 collective-permute-done.10.refs_6_.refs_10_
  33.0 0.4 collective-permute-start.11
  33.3 0.9 collective-permute-done.7.refs_4_.refs_8_
  34.3 1.1 %collective-permute-start.9 = (bf16[896,256]{1,0:T(8,128)(2,1)S(1)}, bf16[896,256]{1,0:T(8,128)(2,1)S(1)}, u32[]{:S(2)}, u32[]{:S(2)}) collective-permute-start(bf16[896,256]{1,0:T(8,128)(2,1)S(1)} %collective-permute-done.7.refs_4_.refs_8_), channel_id=1, source_target_pairs={{0,8},{8,0},{16,24},{24,16},{32,40},{40,32},{48,56},{56,48},{64,72... | collective-permute-start | bytes 1376264 | tf_op jit(solution)/shard_map/ppermute | solution.py:392
  35.4 1.0 %collective-permute-start.14 = (bf16[896,256]{1,0:T(8,128)(2,1)S(1)}, bf16[896,256]{1,0:T(8,128)(2,1)S(1)}, u32[]{:S(2)}, u32[]{:S(2)}) collective-permute-start(bf16[896,256]{1,0:T(8,128)(2,1)S(1)} %collective-permute-done.10.refs_6_.refs_10_), channel_id=1, source_target_pairs={{0,224},{8,232},{16,240},{24,248},{32,0},{40,8},{48,16},{56,24},{6... | collective-permute-start | bytes 1376264 | tf_op jit(solution)/shard_map/ppermute | solution.py:386
  36.4 0.5 collective-permute-start.8
  36.9 0.0 collective-permute-done.11.refs_7_.refs_11_
  36.9 0.0 collective-permute-done.9.refs_5_.refs_9_
  36.9 8.2 %step2.1 = (f32[1792,384]{1,0:T(8,128)S(1)}, f32[896,384]{1,0:T(8,128)S(1)}, bf16[6,128,256]{2,1,0:T(8,128)(2,1)}, f32[8,128]{1,0:T(8,128)}) custom-call(s32[1]{0:T(128)} %bitcast.idx_ref.refs_0_, s32[144]{0:T(256)S(1)} %copy-done.2, ...), custom_call_target="tpu_custom_call", output_to_operand_aliasing={{0}: (12, {}), {1}: (13, {}), {2}: (14, {})} | custom-call | flops 2000000000 | bytes 8000000 | tf_op jit(solution)/shard_map/step2/pallas_call | solution.py:436
  45.1 2.4 %collective-permute-done.14.refs_6_ = bf16[896,256]{1,0:T(8,128)(2,1)S(1)} collective-permute-done((bf16[896,256]{1,0:T(8,128)(2,1)S(1)}, bf16[896,256]{1,0:T(8,128)(2,1)S(1)}, u32[]{:S(2)}, u32[]{:S(2)}) %collective-permute-start.14) | collective-permute-done | bytes 458784 | tf_op jit(solution)/shard_map/ppermute | solution.py:386
  47.5 0.8 collective-permute-start.15
  48.3 0.7 collective-permute-done.8.refs_4_
  49.0 1.6 %collective-permute-start.13 = (bf16[896,256]{1,0:T(8,128)(2,1)S(1)}, bf16[896,256]{1,0:T(8,128)(2,1)S(1)}, u32[]{:S(2)}, u32[]{:S(2)}) collective-permute-start(bf16[896,256]{1,0:T(8,128)(2,1)S(1)} %collective-permute-done.8.refs_4_), channel_id=1, source_target_pairs={{0,8},{8,0},{16,24},{24,16},{32,40},{40,32},{48,56},{56,48},{64,72... | collective-permute-start | bytes 1376264 | tf_op jit(solution)/shard_map/ppermute | solution.py:392
  50.6 0.1 collective-permute-start.12
  50.7 2.7 %collective-permute-start.19 = (bf16[576,256]{1,0:T(8,128)(2,1)S(1)}, bf16[576,256]{1,0:T(8,128)(2,1)S(1)}, u32[]{:S(2)}, u32[]{:S(2)}) collective-permute-start(bf16[576,256]{1,0:T(8,128)(2,1)S(1)} %pad_maximum_fusion.2), channel_id=1, source_target_pairs={{0,224},{8,232},{16,240},{24,248},{32,0},{40,8},{48,16},{56,24},{6... | collective-permute-start | bytes 884744 | tf_op jit(solution)/shard_map/ppermute | solution.py:386
  53.5 0.0 collective-permute-done.15.refs_7_
  53.5 0.0 collective-permute-done.13.refs_5_
  53.5 8.5 %step3.1 = (f32[1792,384]{1,0:T(8,128)S(1)}, f32[896,384]{1,0:T(8,128)S(1)}, bf16[6,128,256]{2,1,0:T(8,128)(2,1)}, f32[8,128]{1,0:T(8,128)}) custom-call(s32[1]{0:T(128)} %bitcast.idx_ref.refs_0_, s32[144]{0:T(256)S(1)} %copy-done.2, ...), custom_call_target="tpu_custom_call", output_to_operand_aliasing={{0}: (12, {}), {1}: (13, {}), {2}: (14, {})} | custom-call | flops 2000000000 | bytes 8000000 | tf_op jit(solution)/shard_map/step3/pallas_call | solution.py:436
  61.9 0.0 collective-permute-done.12.refs_0_.fa.g_ref
  61.9 0.7 collective-permute-start.16
  62.6 0.0 collective-permute-done.19.refs_2_.fb
  62.6 0.1 collective-permute-start.22
  62.7 1.5 %collective-permute-start.20 = (bf16[192,256]{1,0:T(8,128)(2,1)S(1)}, bf16[192,256]{1,0:T(8,128)(2,1)S(1)}, u32[]{:S(2)}, u32[]{:S(2)}) collective-permute-start(bf16[192,256]{1,0:T(8,128)(2,1)S(1)} %slice.24), channel_id=1, source_target_pairs={{0,224},{8,232},{16,240},{24,248},{32,0},{40,8},{48,16},{56,24},{6... | collective-permute-start | bytes 294920 | tf_op jit(solution)/shard_map/ppermute | solution.py:386
  64.2 0.1 collective-permute-start.17
  64.3 0.0 collective-permute-done.22.refs_3_.fbc
  64.3 0.0 collective-permute-done.16.refs_1_.fac.gc_ref
  64.3 1.3 %ext4.1 = (f32[896,384]{1,0:T(8,128)S(1)}, bf16[448,256]{1,0:T(8,128)(2,1)S(1)}) custom-call(s32[1]{0:T(128)} %bitcast.idx_ref.refs_0_, bf16[896,128]{1,0:T(8,128)(2,1)S(1)} %get-tuple-element.35.refs_3_.qx_ref, bf16[640,256]{1,0:T(8,128)(2,1)S(1)} %collective-permute-done.12.refs_0_.fa.g_ref, ...), custom_call_target="tpu_custom_call", output_to_operand_aliasing={{0}: (6, {})} | custom-call | flops 300000000 | bytes 3000000 | tf_op jit(solution)/shard_map/ext4/pallas_call | solution.py:461
  65.6 0.3 collective-permute-start.23
  65.9 2.6 %collective-permute-done.17.ra_ref = bf16[128,256]{1,0:T(8,128)(2,1)S(1)} collective-permute-done((bf16[128,256]{1,0:T(8,128)(2,1)S(1)}, bf16[128,256]{1,0:T(8,128)(2,1)S(1)}, u32[]{:S(2)}, u32[]{:S(2)}) %collective-permute-start.17) | collective-permute-done | bytes 65568 | tf_op jit(solution)/shard_map/ppermute | solution.py:386
  68.5 1.4 %collective-permute-start.18 = (bf16[128,256]{1,0:T(8,128)(2,1)S(1)}, bf16[128,256]{1,0:T(8,128)(2,1)S(1)}, u32[]{:S(2)}, u32[]{:S(2)}) collective-permute-start(bf16[128,256]{1,0:T(8,128)(2,1)S(1)} %collective-permute-done.17.ra_ref), channel_id=1, source_target_pairs={{0,8},{8,0},{16,24},{24,16},{32,40},{40,32},{48,56},{56,48},{64,72... | collective-permute-start | bytes 196616 | tf_op jit(solution)/shard_map/ppermute | solution.py:392
  69.9 0.0 collective-permute-done.20.rb_ref
  70.0 0.0 collective-permute-start.21
  70.0 4.9 %prompt4.1 = (f32[1792,384]{1,0:T(8,128)S(1)}, bf16[6,128,256]{2,1,0:T(8,128)(2,1)}) custom-call(s32[1]{0:T(128)} %bitcast.idx_ref.refs_0_, s32[144]{0:T(256)S(1)} %copy-done.2, bf16[1792,128]{1,0:T(8,128)(2,1)S(1)} %get-tuple-element.32.refs_2_.qs_ref, ...), custom_call_target="tpu_custom_call", output_to_operand_aliasing={{0}: (11, {}), {1}: (12, {})} | custom-call | flops 2000000000 | bytes 6000000 | tf_op jit(solution)/shard_map/prompt4/pallas_call | solution.py:473
  74.9 0.0 collective-permute-done.18.rac_ref
  74.9 0.0 collective-permute-done.21.rbc_ref
  74.9 0.0 collective-permute-done.23.got_ref
  74.9 3.6 %last.1 = (bf16[320,896]{1,0:T(8,128)(2,1)S(1)}, bf16[6,128,256]{2,1,0:T(8,128)(2,1)}) custom-call(s32[1]{0:T(128)} %bitcast.idx_ref.refs_0_, s32[144]{0:T(256)S(1)} %copy-done.2, bf16[1792,128]{1,0:T(8,128)(2,1)S(1)} %get-tuple-element.32.refs_2_.qs_ref, ...), custom_call_target="tpu_custom_call", output_to_operand_aliasing={{1}: (12, {})} | custom-call | flops 500000000 | bytes 4000000 | tf_op jit(solution)/shard_map/last/pallas_call | solution.py:484
  78.6 17.4 %all_to_all.19 = bf16[8,40,896]{2,1,0:T(8,128)(2,1)S(1)} all-to-all(bf16[8,40,896]{2,1,0:T(8,128)(2,1)S(1)} %bitcast.11), channel_id=1, replica_groups=mesh['ctx'=32,'tp'=8] {'tp'}, dimensions={0} | all-to-all | bytes 1146880 | tf_op jit(solution)/shard_map/all_to_all | solution.py:495
  96.0 0.9 copy.20
  (9 shorter events, 0.1 us)
Async XLA Ops:
  2.6 9.0 %collective-permute-start.1 = (bf16[576,256]{1,0:T(8,128)(2,1)S(1)}, bf16[576,256]{1,0:T(8,128)(2,1)S(1)}, u32[]{:S(2)}, u32[]{:S(2)}) collective-permute-start(bf16[576,256]{1,0:T(8,128)(2,1)S(1)} %get-tuple-element.31), channel_id=1, source_target_pairs={{0,16},{8,24},{16,0},{24,8},{32,48},{40,56},{48,32},{56,40},{64,80... | collective-permute-start | bytes 884744 | tf_op jit(solution)/shard_map/ppermute | solution.py:389
  4.8 12.0 %collective-permute-start.3 = (bf16[576,256]{1,0:T(8,128)(2,1)S(1)}, bf16[576,256]{1,0:T(8,128)(2,1)S(1)}, u32[]{:S(2)}, u32[]{:S(2)}) collective-permute-start(bf16[576,256]{1,0:T(8,128)(2,1)S(1)} %get-tuple-element.30.x_ref), channel_id=1, source_target_pairs={{0,32},{8,40},{16,48},{24,56},{32,64},{40,72},{48,80},{56,88},{64,... | collective-permute-start | bytes 884744 | tf_op jit(solution)/shard_map/ppermute | solution.py:386
  6.5 11.9 %collective-permute-start.5 = (bf16[576,256]{1,0:T(8,128)(2,1)S(1)}, bf16[576,256]{1,0:T(8,128)(2,1)S(1)}, u32[]{:S(2)}, u32[]{:S(2)}) collective-permute-start(bf16[576,256]{1,0:T(8,128)(2,1)S(1)} %get-tuple-element.30.x_ref), channel_id=1, source_target_pairs={{0,224},{8,232},{16,240},{24,248},{32,0},{40,8},{48,16},{56,24},{6... | collective-permute-start | bytes 884744 | tf_op jit(solution)/shard_map/ppermute | solution.py:386
  10.4 10.8 %collective-permute-start = (bf16[576,256]{1,0:T(8,128)(2,1)S(1)}, bf16[576,256]{1,0:T(8,128)(2,1)S(1)}, u32[]{:S(2)}, u32[]{:S(2)}) collective-permute-start(bf16[576,256]{1,0:T(8,128)(2,1)S(1)} %get-tuple-element.30.x_ref), channel_id=1, source_target_pairs={{0,8},{8,0},{16,24},{24,16},{32,40},{40,32},{48,56},{56,48},{64,72... | collective-permute-start | bytes 884744 | tf_op jit(solution)/shard_map/ppermute | solution.py:392
  11.7 9.6 %collective-permute-start.2 = (bf16[576,256]{1,0:T(8,128)(2,1)S(1)}, bf16[576,256]{1,0:T(8,128)(2,1)S(1)}, u32[]{:S(2)}, u32[]{:S(2)}) collective-permute-start(bf16[576,256]{1,0:T(8,128)(2,1)S(1)} %collective-permute-done.1.y_ref), channel_id=1, source_target_pairs={{0,8},{8,0},{16,24},{24,16},{32,40},{40,32},{48,56},{56,48},{64,72... | collective-permute-start | bytes 884744 | tf_op jit(solution)/shard_map/ppermute | solution.py:392
  16.8 4.4 %collective-permute-start.4 = (bf16[576,256]{1,0:T(8,128)(2,1)S(1)}, bf16[576,256]{1,0:T(8,128)(2,1)S(1)}, u32[]{:S(2)}, u32[]{:S(2)}) collective-permute-start(bf16[576,256]{1,0:T(8,128)(2,1)S(1)} %collective-permute-done.3.a_ref.refs_8_), channel_id=1, source_target_pairs={{0,8},{8,0},{16,24},{24,16},{32,40},{40,32},{48,56},{56,48},{64,72... | collective-permute-start | bytes 884744 | tf_op jit(solution)/shard_map/ppermute | solution.py:392
  18.4 2.9 %collective-permute-start.6 = (bf16[576,256]{1,0:T(8,128)(2,1)S(1)}, bf16[576,256]{1,0:T(8,128)(2,1)S(1)}, u32[]{:S(2)}, u32[]{:S(2)}) collective-permute-start(bf16[576,256]{1,0:T(8,128)(2,1)S(1)} %collective-permute-done.5.b_ref.refs_10_), channel_id=1, source_target_pairs={{0,8},{8,0},{16,24},{24,16},{32,40},{40,32},{48,56},{56,48},{64,72... | collective-permute-start | bytes 884744 | tf_op jit(solution)/shard_map/ppermute | solution.py:392
  18.5 14.5 %collective-permute-start.10 = (bf16[896,256]{1,0:T(8,128)(2,1)S(1)}, bf16[896,256]{1,0:T(8,128)(2,1)S(1)}, u32[]{:S(2)}, u32[]{:S(2)}) collective-permute-start(bf16[896,256]{1,0:T(8,128)(2,1)S(1)} %get-tuple-element.60), channel_id=1, source_target_pairs={{0,224},{8,232},{16,240},{24,248},{32,0},{40,8},{48,16},{56,24},{6... | collective-permute-start | bytes 1376264 | tf_op jit(solution)/shard_map/ppermute | solution.py:386
  21.2 13.0 %collective-permute-start.7 = (bf16[896,256]{1,0:T(8,128)(2,1)S(1)}, bf16[896,256]{1,0:T(8,128)(2,1)S(1)}, u32[]{:S(2)}, u32[]{:S(2)}) collective-permute-start(bf16[896,256]{1,0:T(8,128)(2,1)S(1)} %get-tuple-element.61), channel_id=1, source_target_pairs={{0,32},{8,40},{16,48},{24,56},{32,64},{40,72},{48,80},{56,88},{64,... | collective-permute-start | bytes 1376264 | tf_op jit(solution)/shard_map/ppermute | solution.py:386
  21.3 1.0 %copy-start = (bf16[6,128,1,256]{3,1,2,0:T(8,128)(2,1)S(1)}, bf16[6,128,1,256]{3,1,2,0:T(8,128)(2,1)}, u32[]{:S(2)}) copy-start(bf16[6,128,1,256]{3,1,2,0:T(8,128)(2,1)} %param.10) | copy-start | bytes 1179652
  22.3 0.9 copy-start.1
  23.2 0.7 copy-start.2
  23.8 1.0 %copy-start.3 = (bf16[256,896]{1,0:T(8,128)(2,1)S(1)}, bf16[256,896]{1,0:T(8,128)(2,1)}, u32[]{:S(2)}) copy-start(bf16[256,896]{1,0:T(8,128)(2,1)} %qp_ref.1) | copy-start | bytes 1376260
  33.0 3.9 %collective-permute-start.11 = (bf16[896,256]{1,0:T(8,128)(2,1)S(1)}, bf16[896,256]{1,0:T(8,128)(2,1)S(1)}, u32[]{:S(2)}, u32[]{:S(2)}) collective-permute-start(bf16[896,256]{1,0:T(8,128)(2,1)S(1)} %collective-permute-done.10.refs_6_.refs_10_), channel_id=1, source_target_pairs={{0,8},{8,0},{16,24},{24,16},{32,40},{40,32},{48,56},{56,48},{64,72... | collective-permute-start | bytes 1376264 | tf_op jit(solution)/shard_map/ppermute | solution.py:392
  34.3 2.6 %collective-permute-start.9 = (bf16[896,256]{1,0:T(8,128)(2,1)S(1)}, bf16[896,256]{1,0:T(8,128)(2,1)S(1)}, u32[]{:S(2)}, u32[]{:S(2)}) collective-permute-start(bf16[896,256]{1,0:T(8,128)(2,1)S(1)} %collective-permute-done.7.refs_4_.refs_8_), channel_id=1, source_target_pairs={{0,8},{8,0},{16,24},{24,16},{32,40},{40,32},{48,56},{56,48},{64,72... | collective-permute-start | bytes 1376264 | tf_op jit(solution)/shard_map/ppermute | solution.py:392
  35.4 12.2 %collective-permute-start.14 = (bf16[896,256]{1,0:T(8,128)(2,1)S(1)}, bf16[896,256]{1,0:T(8,128)(2,1)S(1)}, u32[]{:S(2)}, u32[]{:S(2)}) collective-permute-start(bf16[896,256]{1,0:T(8,128)(2,1)S(1)} %collective-permute-done.10.refs_6_.refs_10_), channel_id=1, source_target_pairs={{0,224},{8,232},{16,240},{24,248},{32,0},{40,8},{48,16},{56,24},{6... | collective-permute-start | bytes 1376264 | tf_op jit(solution)/shard_map/ppermute | solution.py:386
  36.4 12.6 %collective-permute-start.8 = (bf16[896,256]{1,0:T(8,128)(2,1)S(1)}, bf16[896,256]{1,0:T(8,128)(2,1)S(1)}, u32[]{:S(2)}, u32[]{:S(2)}) collective-permute-start(bf16[896,256]{1,0:T(8,128)(2,1)S(1)} %collective-permute-done.7.refs_4_.refs_8_), channel_id=1, source_target_pairs={{0,32},{8,40},{16,48},{24,56},{32,64},{40,72},{48,80},{56,88},{64,... | collective-permute-start | bytes 1376264 | tf_op jit(solution)/shard_map/ppermute | solution.py:386
  47.5 5.9 %collective-permute-start.15 = (bf16[896,256]{1,0:T(8,128)(2,1)S(1)}, bf16[896,256]{1,0:T(8,128)(2,1)S(1)}, u32[]{:S(2)}, u32[]{:S(2)}) collective-permute-start(bf16[896,256]{1,0:T(8,128)(2,1)S(1)} %collective-permute-done.14.refs_6_), channel_id=1, source_target_pairs={{0,8},{8,0},{16,24},{24,16},{32,40},{40,32},{48,56},{56,48},{64,72... | collective-permute-start | bytes 1376264 | tf_op jit(solution)/shard_map/ppermute | solution.py:392
  49.0 4.5 %collective-permute-start.13 = (bf16[896,256]{1,0:T(8,128)(2,1)S(1)}, bf16[896,256]{1,0:T(8,128)(2,1)S(1)}, u32[]{:S(2)}, u32[]{:S(2)}) collective-permute-start(bf16[896,256]{1,0:T(8,128)(2,1)S(1)} %collective-permute-done.8.refs_4_), channel_id=1, source_target_pairs={{0,8},{8,0},{16,24},{24,16},{32,40},{40,32},{48,56},{56,48},{64,72... | collective-permute-start | bytes 1376264 | tf_op jit(solution)/shard_map/ppermute | solution.py:392
  50.6 11.3 %collective-permute-start.12 = (bf16[640,256]{1,0:T(8,128)(2,1)S(1)}, bf16[640,256]{1,0:T(8,128)(2,1)S(1)}, u32[]{:S(2)}, u32[]{:S(2)}) collective-permute-start(bf16[640,256]{1,0:T(8,128)(2,1)S(1)} %slice.20), channel_id=1, source_target_pairs={{0,32},{8,40},{16,48},{24,56},{32,64},{40,72},{48,80},{56,88},{64,... | collective-permute-start | bytes 983048 | tf_op jit(solution)/shard_map/ppermute | solution.py:386
  50.7 11.9 %collective-permute-start.19 = (bf16[576,256]{1,0:T(8,128)(2,1)S(1)}, bf16[576,256]{1,0:T(8,128)(2,1)S(1)}, u32[]{:S(2)}, u32[]{:S(2)}) collective-permute-start(bf16[576,256]{1,0:T(8,128)(2,1)S(1)} %pad_maximum_fusion.2), channel_id=1, source_target_pairs={{0,224},{8,232},{16,240},{24,248},{32,0},{40,8},{48,16},{56,24},{6... | collective-permute-start | bytes 884744 | tf_op jit(solution)/shard_map/ppermute | solution.py:386
  61.9 2.3 %collective-permute-start.16 = (bf16[640,256]{1,0:T(8,128)(2,1)S(1)}, bf16[640,256]{1,0:T(8,128)(2,1)S(1)}, u32[]{:S(2)}, u32[]{:S(2)}) collective-permute-start(bf16[640,256]{1,0:T(8,128)(2,1)S(1)} %collective-permute-done.12.refs_0_.fa.g_ref), channel_id=1, source_target_pairs={{0,8},{8,0},{16,24},{24,16},{32,40},{40,32},{48,56},{56,48},{64,72... | collective-permute-start | bytes 983048 | tf_op jit(solution)/shard_map/ppermute | solution.py:392
  62.6 1.7 %collective-permute-start.22 = (bf16[576,256]{1,0:T(8,128)(2,1)S(1)}, bf16[576,256]{1,0:T(8,128)(2,1)S(1)}, u32[]{:S(2)}, u32[]{:S(2)}) collective-permute-start(bf16[576,256]{1,0:T(8,128)(2,1)S(1)} %collective-permute-done.19.refs_2_.fb), channel_id=1, source_target_pairs={{0,8},{8,0},{16,24},{24,16},{32,40},{40,32},{48,56},{56,48},{64,72... | collective-permute-start | bytes 884744 | tf_op jit(solution)/shard_map/ppermute | solution.py:392
  62.7 7.2 %collective-permute-start.20 = (bf16[192,256]{1,0:T(8,128)(2,1)S(1)}, bf16[192,256]{1,0:T(8,128)(2,1)S(1)}, u32[]{:S(2)}, u32[]{:S(2)}) collective-permute-start(bf16[192,256]{1,0:T(8,128)(2,1)S(1)} %slice.24), channel_id=1, source_target_pairs={{0,224},{8,232},{16,240},{24,248},{32,0},{40,8},{48,16},{56,24},{6... | collective-permute-start | bytes 294920 | tf_op jit(solution)/shard_map/ppermute | solution.py:386
  64.2 4.3 %collective-permute-start.17 = (bf16[128,256]{1,0:T(8,128)(2,1)S(1)}, bf16[128,256]{1,0:T(8,128)(2,1)S(1)}, u32[]{:S(2)}, u32[]{:S(2)}) collective-permute-start(bf16[128,256]{1,0:T(8,128)(2,1)S(1)} %slice.21), channel_id=1, source_target_pairs={{0,32},{8,40},{16,48},{24,56},{32,64},{40,72},{48,80},{56,88},{64,... | collective-permute-start | bytes 196616 | tf_op jit(solution)/shard_map/ppermute | solution.py:386
  65.6 9.3 %collective-permute-start.23 = (bf16[448,256]{1,0:T(8,128)(2,1)S(1)}, bf16[448,256]{1,0:T(8,128)(2,1)S(1)}, u32[]{:S(2)}, u32[]{:S(2)}) collective-permute-start(bf16[448,256]{1,0:T(8,128)(2,1)S(1)} %get-tuple-element.54), channel_id=1, source_target_pairs={{0,16},{8,24},{16,0},{24,8},{32,48},{40,56},{48,32},{56,40},{64,80... | collective-permute-start | bytes 688136 | tf_op jit(solution)/shard_map/ppermute | solution.py:389
  68.5 6.4 %collective-permute-start.18 = (bf16[128,256]{1,0:T(8,128)(2,1)S(1)}, bf16[128,256]{1,0:T(8,128)(2,1)S(1)}, u32[]{:S(2)}, u32[]{:S(2)}) collective-permute-start(bf16[128,256]{1,0:T(8,128)(2,1)S(1)} %collective-permute-done.17.ra_ref), channel_id=1, source_target_pairs={{0,8},{8,0},{16,24},{24,16},{32,40},{40,32},{48,56},{56,48},{64,72... | collective-permute-start | bytes 196616 | tf_op jit(solution)/shard_map/ppermute | solution.py:392
  70.0 5.0 %collective-permute-start.21 = (bf16[192,256]{1,0:T(8,128)(2,1)S(1)}, bf16[192,256]{1,0:T(8,128)(2,1)S(1)}, u32[]{:S(2)}, u32[]{:S(2)}) collective-permute-start(bf16[192,256]{1,0:T(8,128)(2,1)S(1)} %collective-permute-done.20.rb_ref), channel_id=1, source_target_pairs={{0,8},{8,0},{16,24},{24,16},{32,40},{40,32},{48,56},{56,48},{64,72... | collective-permute-start | bytes 294920 | tf_op jit(solution)/shard_map/ppermute | solution.py:392

commit v2 on v1

--- a/solution.py
+++ b/solution.py
@@ -261,7 +261,11 @@
     for i in range(2):
         shards = [(before[2 * i], 256), (before[2 * i + 1], 256), (now[2 * i], y_rows[i]), (now[2 * i + 1], y_rows[i])]
         parts.append([((ref, row), (ref, row + 128)) for ref, row in shards])
-    fronts = [ref[row:row + 128, :] for plane in parts for (ref, row), _ in plane]
+    blocks = [(now[i], y_rows[i // 2]) for i in range(4)]
+    blocks += [(now[0], 0), (now[1], 0)] if k == 4 else [(ref, 256) for ref in now]
+    if k == 2:
+        blocks += [(ref, 256) for ref in before]
+    fronts = [ref[row:row + 128, :] for ref, row in blocks]
     update(qs_ref, 896, sp_ref, 896, 128, fronts, source=sp_in)
     selected(z, (minus, plus), qs_ref, sp_ref, kv_ref, parts)
 
@@ -346,7 +350,7 @@
             (shard, rb_ref, None, 0, 128), (shard ^ 1, rbc_ref, None, 0, 128),
         ],
     )
-    firsts = [g_ref[0:128, :], gc_ref[0:128, :], ra_ref[...], rac_ref[...]]
+    firsts = [ra_ref[...], rac_ref[...]]
     sp_ref[0:896, :] = sp_in[0:896, :]
     update(qs_ref, 896, sp_ref, 896, 128, firsts, source=sp_in)
     blocks = [

time: 97.2 us -> 96.5 us (level)
  transfers between devices with their start and end apart: 24 -> 24, of which waited for: 5 -> 5; matrix products, arithmetic and copies ran while one was open for 0% -> 0% of each run, Pallas kernels for 32% -> 33%
where the time goes in v2:
time: 96.5 us; the launch traced here: 96.3 us
  Pallas kernels  36.7 us (38%)
  starting transfers between devices  26.6 us (28%)
  blocking collectives  17.5 us (18%)
  waiting for transfers between devices  10 us (10%)
  local copies, waits for them, and re-layouts  4.53 us (5%)
    all_to_all x1, blocking collectives, body(): lax.all_to_all(local_context, 'tp', split_axis=0, concat_axis=1, tiled=True)  17.5 us
    pallas_call x2, Pallas kernels, step(): pl.pallas_call(lambda *refs: step_body(k, *refs), out_shape=(sp_t, se_t,...  17.4 us
    ppermute x10, starting transfers between devices, shift(): return lax.ppermute(x, 'ctx', [(i, (i + 4 * d) % 32) for i in range(32)])  14.1 us
    ppermute x10, waiting for transfers between devices, shift(): return lax.ppermute(x, 'ctx', [(i, (i + 4 * d) % 32) for i in range(32)])  9.99 us
    ppermute x12, starting transfers between devices, flip_c(): return lax.ppermute(x, 'ctx', [(i, i ^ 1) for i in range(32)])  9.95 us
    pallas_call x1, Pallas kernels, body(): pl.pallas_call(first_body, out_shape=(arr((1792, 128)), arr((896, 128)),...  8.09 us
    pallas_call x1, Pallas kernels, body(): pl.pallas_call(prompt4_body, out_shape=(sp_t, pool_t), in_specs=[SMEM, SM...  4.65 us
    unnamed x8, local copies, waits for them, and re-layouts  3.59 us
  transfers between devices with their start and end apart: 24, of which 5 were waited for; matrix products, arithmetic and copies ran while one was open for 0% of the time, Pallas kernels for 33%

profile of v2, /device:TPU:1, one launch (start us, length us, event | category | flops | bytes accessed | tf_op | source)
XLA Modules:
  0.0 96.3 jit_solution(15018789310157016350)
XLA Ops:
  0.6 2.0 %prep.1 = (bf16[576,256]{1,0:T(8,128)(2,1)S(1)}, bf16[576,256]{1,0:T(8,128)(2,1)S(1)}) custom-call(s32[1]{0:T(128)} %bitcast.idx_ref.refs_0_, s32[144]{0:T(256)} %table_ref.7, bf16[6,128,256]{2,1,0:T(8,128)(2,1)} %bitcast.12, bf16[256,256]{1,0:T(8,128)(2,1)} %bitcast.17, bf16[64,256]{1,0:T(8,128)(2,1)} %bitcast.18, bf16[64,896]{1,0:T(8,128)(2,1)} %qe_ref.3), custom_call_target="tpu_custom_call" | custom-call | tf_op jit(solution)/shard_map/prep/pallas_call | solution.py:407
  2.6 2.2 %collective-permute-start.1 = (bf16[576,256]{1,0:T(8,128)(2,1)S(1)}, bf16[576,256]{1,0:T(8,128)(2,1)S(1)}, u32[]{:S(2)}, u32[]{:S(2)}) collective-permute-start(bf16[576,256]{1,0:T(8,128)(2,1)S(1)} %get-tuple-element.31), channel_id=1, source_target_pairs={{0,16},{8,24},{16,0},{24,8},{32,48},{40,56},{48,32},{56,40},{64,80... | collective-permute-start | bytes 884744 | tf_op jit(solution)/shard_map/ppermute | solution.py:393
  4.8 1.6 %collective-permute-start.3 = (bf16[576,256]{1,0:T(8,128)(2,1)S(1)}, bf16[576,256]{1,0:T(8,128)(2,1)S(1)}, u32[]{:S(2)}, u32[]{:S(2)}) collective-permute-start(bf16[576,256]{1,0:T(8,128)(2,1)S(1)} %get-tuple-element.30.x_ref), channel_id=1, source_target_pairs={{0,32},{8,40},{16,48},{24,56},{32,64},{40,72},{48,80},{56,88},{64,... | collective-permute-start | bytes 884744 | tf_op jit(solution)/shard_map/ppermute | solution.py:390
  6.5 3.9 %collective-permute-start.5 = (bf16[576,256]{1,0:T(8,128)(2,1)S(1)}, bf16[576,256]{1,0:T(8,128)(2,1)S(1)}, u32[]{:S(2)}, u32[]{:S(2)}) collective-permute-start(bf16[576,256]{1,0:T(8,128)(2,1)S(1)} %get-tuple-element.30.x_ref), channel_id=1, source_target_pairs={{0,224},{8,232},{16,240},{24,248},{32,0},{40,8},{48,16},{56,24},{6... | collective-permute-start | bytes 884744 | tf_op jit(solution)/shard_map/ppermute | solution.py:390
  10.4 1.2 %collective-permute-start = (bf16[576,256]{1,0:T(8,128)(2,1)S(1)}, bf16[576,256]{1,0:T(8,128)(2,1)S(1)}, u32[]{:S(2)}, u32[]{:S(2)}) collective-permute-start(bf16[576,256]{1,0:T(8,128)(2,1)S(1)} %get-tuple-element.30.x_ref), channel_id=1, source_target_pairs={{0,8},{8,0},{16,24},{24,16},{32,40},{40,32},{48,56},{56,48},{64,72... | collective-permute-start | bytes 884744 | tf_op jit(solution)/shard_map/ppermute | solution.py:396
  11.7 0.0 collective-permute-done.1.y_ref
  11.7 1.1 %collective-permute-start.2 = (bf16[576,256]{1,0:T(8,128)(2,1)S(1)}, bf16[576,256]{1,0:T(8,128)(2,1)S(1)}, u32[]{:S(2)}, u32[]{:S(2)}) collective-permute-start(bf16[576,256]{1,0:T(8,128)(2,1)S(1)} %collective-permute-done.1.y_ref), channel_id=1, source_target_pairs={{0,8},{8,0},{16,24},{24,16},{32,40},{40,32},{48,56},{56,48},{64,72... | collective-permute-start | bytes 884744 | tf_op jit(solution)/shard_map/ppermute | solution.py:396
  12.8 4.0 %collective-permute-done.3.a_ref.refs_8_ = bf16[576,256]{1,0:T(8,128)(2,1)S(1)} collective-permute-done((bf16[576,256]{1,0:T(8,128)(2,1)S(1)}, bf16[576,256]{1,0:T(8,128)(2,1)S(1)}, u32[]{:S(2)}, u32[]{:S(2)}) %collective-permute-start.3) | collective-permute-done | bytes 294944 | tf_op jit(solution)/shard_map/ppermute | solution.py:390
  16.8 1.5 %collective-permute-start.4 = (bf16[576,256]{1,0:T(8,128)(2,1)S(1)}, bf16[576,256]{1,0:T(8,128)(2,1)S(1)}, u32[]{:S(2)}, u32[]{:S(2)}) collective-permute-start(bf16[576,256]{1,0:T(8,128)(2,1)S(1)} %collective-permute-done.3.a_ref.refs_8_), channel_id=1, source_target_pairs={{0,8},{8,0},{16,24},{24,16},{32,40},{40,32},{48,56},{56,48},{64,72... | collective-permute-start | bytes 884744 | tf_op jit(solution)/shard_map/ppermute | solution.py:396
  18.4 0.0 collective-permute-done.5.b_ref.refs_10_
  18.4 0.0 collective-permute-start.6
  18.4 0.1 pad_maximum_fusion
  18.5 2.7 %collective-permute-start.10 = (bf16[896,256]{1,0:T(8,128)(2,1)S(1)}, bf16[896,256]{1,0:T(8,128)(2,1)S(1)}, u32[]{:S(2)}, u32[]{:S(2)}) collective-permute-start(bf16[896,256]{1,0:T(8,128)(2,1)S(1)} %get-tuple-element.60), channel_id=1, source_target_pairs={{0,224},{8,232},{16,240},{24,248},{32,0},{40,8},{48,16},{56,24},{6... | collective-permute-start | bytes 1376264 | tf_op jit(solution)/shard_map/ppermute | solution.py:390
  21.2 0.0 collective-permute-done.xc_ref
  21.2 0.0 collective-permute-start.7
  21.2 0.0 collective-permute-done.4.ac_ref.refs_9_
  21.2 0.0 collective-permute-done.6.bc_ref.refs_11_
  21.3 0.0 collective-permute-done.2.yc_ref
  21.3 0.0 copy-start
  21.3 1.0 %copy-done = bf16[6,128,1,256]{3,1,2,0:T(8,128)(2,1)S(1)} copy-done((bf16[6,128,1,256]{3,1,2,0:T(8,128)(2,1)S(1)}, bf16[6,128,1,256]{3,1,2,0:T(8,128)(2,1)}, u32[]{:S(2)}) %copy-start) | copy-done | bytes 393240
  22.3 0.0 copy-start.1
  22.3 0.9 copy-done.1
  23.2 0.7 copy-done.2
  23.8 1.0 %copy-done.3 = bf16[256,896]{1,0:T(8,128)(2,1)S(1)} copy-done((bf16[256,896]{1,0:T(8,128)(2,1)S(1)}, bf16[256,896]{1,0:T(8,128)(2,1)}, u32[]{:S(2)}) %copy-start.3) | copy-done | bytes 458776
  24.9 8.1 %step1.1 = (bf16[1792,128]{1,0:T(8,128)(2,1)S(1)}, bf16[896,128]{1,0:T(8,128)(2,1)S(1)}, f32[1792,384]{1,0:T(8,128)S(1)}, f32[896,384]{1,0:T(8,128)S(1)}, bf16[6...) custom-call(s32[1]{0:T(128)} %bitcast.idx_ref.refs_0_, s32[144]{0:T(256)S(1)} %copy-done.2, bf16[256,896]{1,0:T(8,128)(2,1)S(1)} %copy-done.3, ...), custom_call_target="tpu_custom_call" | custom-call | flops 2000000000 | bytes 4000000 | tf_op jit(solution)/shard_map/step1/pallas_call | solution.py:428
  33.0 0.0 collective-permute-done.10.refs_6_.refs_10_
  33.0 0.4 collective-permute-start.11
  33.3 0.9 collective-permute-done.7.refs_4_.refs_8_
  34.3 1.1 %collective-permute-start.9 = (bf16[896,256]{1,0:T(8,128)(2,1)S(1)}, bf16[896,256]{1,0:T(8,128)(2,1)S(1)}, u32[]{:S(2)}, u32[]{:S(2)}) collective-permute-start(bf16[896,256]{1,0:T(8,128)(2,1)S(1)} %collective-permute-done.7.refs_4_.refs_8_), channel_id=1, source_target_pairs={{0,8},{8,0},{16,24},{24,16},{32,40},{40,32},{48,56},{56,48},{64,72... | collective-permute-start | bytes 1376264 | tf_op jit(solution)/shard_map/ppermute | solution.py:396
  35.4 1.0 %collective-permute-start.14 = (bf16[896,256]{1,0:T(8,128)(2,1)S(1)}, bf16[896,256]{1,0:T(8,128)(2,1)S(1)}, u32[]{:S(2)}, u32[]{:S(2)}) collective-permute-start(bf16[896,256]{1,0:T(8,128)(2,1)S(1)} %collective-permute-done.10.refs_6_.refs_10_), channel_id=1, source_target_pairs={{0,224},{8,232},{16,240},{24,248},{32,0},{40,8},{48,16},{56,24},{6... | collective-permute-start | bytes 1376264 | tf_op jit(solution)/shard_map/ppermute | solution.py:390
  36.4 0.5 collective-permute-start.8
  36.9 0.0 collective-permute-done.11.refs_7_.refs_11_
  36.9 0.0 collective-permute-done.9.refs_5_.refs_9_
  36.9 8.9 %step2.1 = (f32[1792,384]{1,0:T(8,128)S(1)}, f32[896,384]{1,0:T(8,128)S(1)}, bf16[6,128,256]{2,1,0:T(8,128)(2,1)}, f32[8,128]{1,0:T(8,128)}) custom-call(s32[1]{0:T(128)} %bitcast.idx_ref.refs_0_, s32[144]{0:T(256)S(1)} %copy-done.2, ...), custom_call_target="tpu_custom_call", output_to_operand_aliasing={{0}: (12, {}), {1}: (13, {}), {2}: (14, {})} | custom-call | flops 2000000000 | bytes 8000000 | tf_op jit(solution)/shard_map/step2/pallas_call | solution.py:440
  45.8 1.8 %collective-permute-done.14.refs_6_ = bf16[896,256]{1,0:T(8,128)(2,1)S(1)} collective-permute-done((bf16[896,256]{1,0:T(8,128)(2,1)S(1)}, bf16[896,256]{1,0:T(8,128)(2,1)S(1)}, u32[]{:S(2)}, u32[]{:S(2)}) %collective-permute-start.14) | collective-permute-done | bytes 458784 | tf_op jit(solution)/shard_map/ppermute | solution.py:390
  47.5 0.8 collective-permute-start.15
  48.3 0.7 collective-permute-done.8.refs_4_
  49.0 1.6 %collective-permute-start.13 = (bf16[896,256]{1,0:T(8,128)(2,1)S(1)}, bf16[896,256]{1,0:T(8,128)(2,1)S(1)}, u32[]{:S(2)}, u32[]{:S(2)}) collective-permute-start(bf16[896,256]{1,0:T(8,128)(2,1)S(1)} %collective-permute-done.8.refs_4_), channel_id=1, source_target_pairs={{0,8},{8,0},{16,24},{24,16},{32,40},{40,32},{48,56},{56,48},{64,72... | collective-permute-start | bytes 1376264 | tf_op jit(solution)/shard_map/ppermute | solution.py:396
  50.6 0.1 collective-permute-start.12
  50.7 2.7 %collective-permute-start.19 = (bf16[576,256]{1,0:T(8,128)(2,1)S(1)}, bf16[576,256]{1,0:T(8,128)(2,1)S(1)}, u32[]{:S(2)}, u32[]{:S(2)}) collective-permute-start(bf16[576,256]{1,0:T(8,128)(2,1)S(1)} %pad_maximum_fusion.2), channel_id=1, source_target_pairs={{0,224},{8,232},{16,240},{24,248},{32,0},{40,8},{48,16},{56,24},{6... | collective-permute-start | bytes 884744 | tf_op jit(solution)/shard_map/ppermute | solution.py:390
  53.5 0.0 collective-permute-done.15.refs_7_
  53.5 0.0 collective-permute-done.13.refs_5_
  53.5 8.5 %step3.1 = (f32[1792,384]{1,0:T(8,128)S(1)}, f32[896,384]{1,0:T(8,128)S(1)}, bf16[6,128,256]{2,1,0:T(8,128)(2,1)}, f32[8,128]{1,0:T(8,128)}) custom-call(s32[1]{0:T(128)} %bitcast.idx_ref.refs_0_, s32[144]{0:T(256)S(1)} %copy-done.2, ...), custom_call_target="tpu_custom_call", output_to_operand_aliasing={{0}: (12, {}), {1}: (13, {}), {2}: (14, {})} | custom-call | flops 2000000000 | bytes 8000000 | tf_op jit(solution)/shard_map/step3/pallas_call | solution.py:440
  61.9 0.0 collective-permute-done.12.refs_0_.fa.g_ref
  61.9 0.7 collective-permute-start.16
  62.6 0.0 collective-permute-done.19.refs_2_.fb
  62.6 0.1 collective-permute-start.22
  62.7 1.5 %collective-permute-start.20 = (bf16[192,256]{1,0:T(8,128)(2,1)S(1)}, bf16[192,256]{1,0:T(8,128)(2,1)S(1)}, u32[]{:S(2)}, u32[]{:S(2)}) collective-permute-start(bf16[192,256]{1,0:T(8,128)(2,1)S(1)} %slice.24), channel_id=1, source_target_pairs={{0,224},{8,232},{16,240},{24,248},{32,0},{40,8},{48,16},{56,24},{6... | collective-permute-start | bytes 294920 | tf_op jit(solution)/shard_map/ppermute | solution.py:390
  64.2 0.1 collective-permute-start.17
  64.3 0.0 collective-permute-done.22.refs_3_.fbc
  64.3 0.0 collective-permute-done.16.refs_1_.fac.gc_ref
  64.3 1.3 %ext4.1 = (f32[896,384]{1,0:T(8,128)S(1)}, bf16[448,256]{1,0:T(8,128)(2,1)S(1)}) custom-call(s32[1]{0:T(128)} %bitcast.idx_ref.refs_0_, bf16[896,128]{1,0:T(8,128)(2,1)S(1)} %get-tuple-element.35.refs_3_.qx_ref, bf16[640,256]{1,0:T(8,128)(2,1)S(1)} %collective-permute-done.12.refs_0_.fa.g_ref, ...), custom_call_target="tpu_custom_call", output_to_operand_aliasing={{0}: (6, {})} | custom-call | flops 300000000 | bytes 3000000 | tf_op jit(solution)/shard_map/ext4/pallas_call | solution.py:465
  65.6 0.3 collective-permute-start.23
  65.9 2.6 %collective-permute-done.17.ra_ref = bf16[128,256]{1,0:T(8,128)(2,1)S(1)} collective-permute-done((bf16[128,256]{1,0:T(8,128)(2,1)S(1)}, bf16[128,256]{1,0:T(8,128)(2,1)S(1)}, u32[]{:S(2)}, u32[]{:S(2)}) %collective-permute-start.17) | collective-permute-done | bytes 65568 | tf_op jit(solution)/shard_map/ppermute | solution.py:390
  68.5 1.4 %collective-permute-start.18 = (bf16[128,256]{1,0:T(8,128)(2,1)S(1)}, bf16[128,256]{1,0:T(8,128)(2,1)S(1)}, u32[]{:S(2)}, u32[]{:S(2)}) collective-permute-start(bf16[128,256]{1,0:T(8,128)(2,1)S(1)} %collective-permute-done.17.ra_ref), channel_id=1, source_target_pairs={{0,8},{8,0},{16,24},{24,16},{32,40},{40,32},{48,56},{56,48},{64,72... | collective-permute-start | bytes 196616 | tf_op jit(solution)/shard_map/ppermute | solution.py:396
  69.9 0.0 collective-permute-done.20.rb_ref
  70.0 0.0 collective-permute-start.21
  70.0 4.7 %prompt4.1 = (f32[1792,384]{1,0:T(8,128)S(1)}, bf16[6,128,256]{2,1,0:T(8,128)(2,1)}) custom-call(s32[1]{0:T(128)} %bitcast.idx_ref.refs_0_, s32[144]{0:T(256)S(1)} %copy-done.2, bf16[1792,128]{1,0:T(8,128)(2,1)S(1)} %get-tuple-element.32.refs_2_.qs_ref, ...), custom_call_target="tpu_custom_call", output_to_operand_aliasing={{0}: (11, {}), {1}: (12, {})} | custom-call | flops 2000000000 | bytes 6000000 | tf_op jit(solution)/shard_map/prompt4/pallas_call | solution.py:477
  74.6 0.0 collective-permute-done.18.rac_ref
  74.6 0.0 collective-permute-done.21.rbc_ref
  74.6 0.0 collective-permute-done.23.got_ref
  74.6 3.3 %last.1 = (bf16[320,896]{1,0:T(8,128)(2,1)S(1)}, bf16[6,128,256]{2,1,0:T(8,128)(2,1)}) custom-call(s32[1]{0:T(128)} %bitcast.idx_ref.refs_0_, s32[144]{0:T(256)S(1)} %copy-done.2, bf16[1792,128]{1,0:T(8,128)(2,1)S(1)} %get-tuple-element.32.refs_2_.qs_ref, ...), custom_call_target="tpu_custom_call", output_to_operand_aliasing={{1}: (12, {})} | custom-call | flops 500000000 | bytes 4000000 | tf_op jit(solution)/shard_map/last/pallas_call | solution.py:488
  77.9 17.5 %all_to_all.19 = bf16[8,40,896]{2,1,0:T(8,128)(2,1)S(1)} all-to-all(bf16[8,40,896]{2,1,0:T(8,128)(2,1)S(1)} %bitcast.11), channel_id=1, replica_groups=mesh['ctx'=32,'tp'=8] {'tp'}, dimensions={0} | all-to-all | bytes 1146880 | tf_op jit(solution)/shard_map/all_to_all | solution.py:499
  95.4 0.9 copy.20
  (9 shorter events, 0.1 us)
Async XLA Ops:
  2.6 9.0 %collective-permute-start.1 = (bf16[576,256]{1,0:T(8,128)(2,1)S(1)}, bf16[576,256]{1,0:T(8,128)(2,1)S(1)}, u32[]{:S(2)}, u32[]{:S(2)}) collective-permute-start(bf16[576,256]{1,0:T(8,128)(2,1)S(1)} %get-tuple-element.31), channel_id=1, source_target_pairs={{0,16},{8,24},{16,0},{24,8},{32,48},{40,56},{48,32},{56,40},{64,80... | collective-permute-start | bytes 884744 | tf_op jit(solution)/shard_map/ppermute | solution.py:393
  4.8 12.0 %collective-permute-start.3 = (bf16[576,256]{1,0:T(8,128)(2,1)S(1)}, bf16[576,256]{1,0:T(8,128)(2,1)S(1)}, u32[]{:S(2)}, u32[]{:S(2)}) collective-permute-start(bf16[576,256]{1,0:T(8,128)(2,1)S(1)} %get-tuple-element.30.x_ref), channel_id=1, source_target_pairs={{0,32},{8,40},{16,48},{24,56},{32,64},{40,72},{48,80},{56,88},{64,... | collective-permute-start | bytes 884744 | tf_op jit(solution)/shard_map/ppermute | solution.py:390
  6.5 11.9 %collective-permute-start.5 = (bf16[576,256]{1,0:T(8,128)(2,1)S(1)}, bf16[576,256]{1,0:T(8,128)(2,1)S(1)}, u32[]{:S(2)}, u32[]{:S(2)}) collective-permute-start(bf16[576,256]{1,0:T(8,128)(2,1)S(1)} %get-tuple-element.30.x_ref), channel_id=1, source_target_pairs={{0,224},{8,232},{16,240},{24,248},{32,0},{40,8},{48,16},{56,24},{6... | collective-permute-start | bytes 884744 | tf_op jit(solution)/shard_map/ppermute | solution.py:390
  10.4 10.8 %collective-permute-start = (bf16[576,256]{1,0:T(8,128)(2,1)S(1)}, bf16[576,256]{1,0:T(8,128)(2,1)S(1)}, u32[]{:S(2)}, u32[]{:S(2)}) collective-permute-start(bf16[576,256]{1,0:T(8,128)(2,1)S(1)} %get-tuple-element.30.x_ref), channel_id=1, source_target_pairs={{0,8},{8,0},{16,24},{24,16},{32,40},{40,32},{48,56},{56,48},{64,72... | collective-permute-start | bytes 884744 | tf_op jit(solution)/shard_map/ppermute | solution.py:396
  11.7 9.6 %collective-permute-start.2 = (bf16[576,256]{1,0:T(8,128)(2,1)S(1)}, bf16[576,256]{1,0:T(8,128)(2,1)S(1)}, u32[]{:S(2)}, u32[]{:S(2)}) collective-permute-start(bf16[576,256]{1,0:T(8,128)(2,1)S(1)} %collective-permute-done.1.y_ref), channel_id=1, source_target_pairs={{0,8},{8,0},{16,24},{24,16},{32,40},{40,32},{48,56},{56,48},{64,72... | collective-permute-start | bytes 884744 | tf_op jit(solution)/shard_map/ppermute | solution.py:396
  16.8 4.4 %collective-permute-start.4 = (bf16[576,256]{1,0:T(8,128)(2,1)S(1)}, bf16[576,256]{1,0:T(8,128)(2,1)S(1)}, u32[]{:S(2)}, u32[]{:S(2)}) collective-permute-start(bf16[576,256]{1,0:T(8,128)(2,1)S(1)} %collective-permute-done.3.a_ref.refs_8_), channel_id=1, source_target_pairs={{0,8},{8,0},{16,24},{24,16},{32,40},{40,32},{48,56},{56,48},{64,72... | collective-permute-start | bytes 884744 | tf_op jit(solution)/shard_map/ppermute | solution.py:396
  18.4 2.9 %collective-permute-start.6 = (bf16[576,256]{1,0:T(8,128)(2,1)S(1)}, bf16[576,256]{1,0:T(8,128)(2,1)S(1)}, u32[]{:S(2)}, u32[]{:S(2)}) collective-permute-start(bf16[576,256]{1,0:T(8,128)(2,1)S(1)} %collective-permute-done.5.b_ref.refs_10_), channel_id=1, source_target_pairs={{0,8},{8,0},{16,24},{24,16},{32,40},{40,32},{48,56},{56,48},{64,72... | collective-permute-start | bytes 884744 | tf_op jit(solution)/shard_map/ppermute | solution.py:396
  18.5 14.5 %collective-permute-start.10 = (bf16[896,256]{1,0:T(8,128)(2,1)S(1)}, bf16[896,256]{1,0:T(8,128)(2,1)S(1)}, u32[]{:S(2)}, u32[]{:S(2)}) collective-permute-start(bf16[896,256]{1,0:T(8,128)(2,1)S(1)} %get-tuple-element.60), channel_id=1, source_target_pairs={{0,224},{8,232},{16,240},{24,248},{32,0},{40,8},{48,16},{56,24},{6... | collective-permute-start | bytes 1376264 | tf_op jit(solution)/shard_map/ppermute | solution.py:390
  21.2 13.0 %collective-permute-start.7 = (bf16[896,256]{1,0:T(8,128)(2,1)S(1)}, bf16[896,256]{1,0:T(8,128)(2,1)S(1)}, u32[]{:S(2)}, u32[]{:S(2)}) collective-permute-start(bf16[896,256]{1,0:T(8,128)(2,1)S(1)} %get-tuple-element.61), channel_id=1, source_target_pairs={{0,32},{8,40},{16,48},{24,56},{32,64},{40,72},{48,80},{56,88},{64,... | collective-permute-start | bytes 1376264 | tf_op jit(solution)/shard_map/ppermute | solution.py:390
  21.3 1.0 %copy-start = (bf16[6,128,1,256]{3,1,2,0:T(8,128)(2,1)S(1)}, bf16[6,128,1,256]{3,1,2,0:T(8,128)(2,1)}, u32[]{:S(2)}) copy-start(bf16[6,128,1,256]{3,1,2,0:T(8,128)(2,1)} %param.10) | copy-start | bytes 1179652
  22.3 0.9 copy-start.1
  23.2 0.7 copy-start.2
  23.8 1.0 %copy-start.3 = (bf16[256,896]{1,0:T(8,128)(2,1)S(1)}, bf16[256,896]{1,0:T(8,128)(2,1)}, u32[]{:S(2)}) copy-start(bf16[256,896]{1,0:T(8,128)(2,1)} %qp_ref.1) | copy-start | bytes 1376260
  33.0 3.9 %collective-permute-start.11 = (bf16[896,256]{1,0:T(8,128)(2,1)S(1)}, bf16[896,256]{1,0:T(8,128)(2,1)S(1)}, u32[]{:S(2)}, u32[]{:S(2)}) collective-permute-start(bf16[896,256]{1,0:T(8,128)(2,1)S(1)} %collective-permute-done.10.refs_6_.refs_10_), channel_id=1, source_target_pairs={{0,8},{8,0},{16,24},{24,16},{32,40},{40,32},{48,56},{56,48},{64,72... | collective-permute-start | bytes 1376264 | tf_op jit(solution)/shard_map/ppermute | solution.py:396
  34.3 2.6 %collective-permute-start.9 = (bf16[896,256]{1,0:T(8,128)(2,1)S(1)}, bf16[896,256]{1,0:T(8,128)(2,1)S(1)}, u32[]{:S(2)}, u32[]{:S(2)}) collective-permute-start(bf16[896,256]{1,0:T(8,128)(2,1)S(1)} %collective-permute-done.7.refs_4_.refs_8_), channel_id=1, source_target_pairs={{0,8},{8,0},{16,24},{24,16},{32,40},{40,32},{48,56},{56,48},{64,72... | collective-permute-start | bytes 1376264 | tf_op jit(solution)/shard_map/ppermute | solution.py:396
  35.4 12.2 %collective-permute-start.14 = (bf16[896,256]{1,0:T(8,128)(2,1)S(1)}, bf16[896,256]{1,0:T(8,128)(2,1)S(1)}, u32[]{:S(2)}, u32[]{:S(2)}) collective-permute-start(bf16[896,256]{1,0:T(8,128)(2,1)S(1)} %collective-permute-done.10.refs_6_.refs_10_), channel_id=1, source_target_pairs={{0,224},{8,232},{16,240},{24,248},{32,0},{40,8},{48,16},{56,24},{6... | collective-permute-start | bytes 1376264 | tf_op jit(solution)/shard_map/ppermute | solution.py:390
  36.4 12.6 %collective-permute-start.8 = (bf16[896,256]{1,0:T(8,128)(2,1)S(1)}, bf16[896,256]{1,0:T(8,128)(2,1)S(1)}, u32[]{:S(2)}, u32[]{:S(2)}) collective-permute-start(bf16[896,256]{1,0:T(8,128)(2,1)S(1)} %collective-permute-done.7.refs_4_.refs_8_), channel_id=1, source_target_pairs={{0,32},{8,40},{16,48},{24,56},{32,64},{40,72},{48,80},{56,88},{64,... | collective-permute-start | bytes 1376264 | tf_op jit(solution)/shard_map/ppermute | solution.py:390
  47.5 5.9 %collective-permute-start.15 = (bf16[896,256]{1,0:T(8,128)(2,1)S(1)}, bf16[896,256]{1,0:T(8,128)(2,1)S(1)}, u32[]{:S(2)}, u32[]{:S(2)}) collective-permute-start(bf16[896,256]{1,0:T(8,128)(2,1)S(1)} %collective-permute-done.14.refs_6_), channel_id=1, source_target_pairs={{0,8},{8,0},{16,24},{24,16},{32,40},{40,32},{48,56},{56,48},{64,72... | collective-permute-start | bytes 1376264 | tf_op jit(solution)/shard_map/ppermute | solution.py:396
  49.0 4.5 %collective-permute-start.13 = (bf16[896,256]{1,0:T(8,128)(2,1)S(1)}, bf16[896,256]{1,0:T(8,128)(2,1)S(1)}, u32[]{:S(2)}, u32[]{:S(2)}) collective-permute-start(bf16[896,256]{1,0:T(8,128)(2,1)S(1)} %collective-permute-done.8.refs_4_), channel_id=1, source_target_pairs={{0,8},{8,0},{16,24},{24,16},{32,40},{40,32},{48,56},{56,48},{64,72... | collective-permute-start | bytes 1376264 | tf_op jit(solution)/shard_map/ppermute | solution.py:396
  50.6 11.3 %collective-permute-start.12 = (bf16[640,256]{1,0:T(8,128)(2,1)S(1)}, bf16[640,256]{1,0:T(8,128)(2,1)S(1)}, u32[]{:S(2)}, u32[]{:S(2)}) collective-permute-start(bf16[640,256]{1,0:T(8,128)(2,1)S(1)} %slice.20), channel_id=1, source_target_pairs={{0,32},{8,40},{16,48},{24,56},{32,64},{40,72},{48,80},{56,88},{64,... | collective-permute-start | bytes 983048 | tf_op jit(solution)/shard_map/ppermute | solution.py:390
  50.7 11.9 %collective-permute-start.19 = (bf16[576,256]{1,0:T(8,128)(2,1)S(1)}, bf16[576,256]{1,0:T(8,128)(2,1)S(1)}, u32[]{:S(2)}, u32[]{:S(2)}) collective-permute-start(bf16[576,256]{1,0:T(8,128)(2,1)S(1)} %pad_maximum_fusion.2), channel_id=1, source_target_pairs={{0,224},{8,232},{16,240},{24,248},{32,0},{40,8},{48,16},{56,24},{6... | collective-permute-start | bytes 884744 | tf_op jit(solution)/shard_map/ppermute | solution.py:390
  61.9 2.3 %collective-permute-start.16 = (bf16[640,256]{1,0:T(8,128)(2,1)S(1)}, bf16[640,256]{1,0:T(8,128)(2,1)S(1)}, u32[]{:S(2)}, u32[]{:S(2)}) collective-permute-start(bf16[640,256]{1,0:T(8,128)(2,1)S(1)} %collective-permute-done.12.refs_0_.fa.g_ref), channel_id=1, source_target_pairs={{0,8},{8,0},{16,24},{24,16},{32,40},{40,32},{48,56},{56,48},{64,72... | collective-permute-start | bytes 983048 | tf_op jit(solution)/shard_map/ppermute | solution.py:396
  62.6 1.7 %collective-permute-start.22 = (bf16[576,256]{1,0:T(8,128)(2,1)S(1)}, bf16[576,256]{1,0:T(8,128)(2,1)S(1)}, u32[]{:S(2)}, u32[]{:S(2)}) collective-permute-start(bf16[576,256]{1,0:T(8,128)(2,1)S(1)} %collective-permute-done.19.refs_2_.fb), channel_id=1, source_target_pairs={{0,8},{8,0},{16,24},{24,16},{32,40},{40,32},{48,56},{56,48},{64,72... | collective-permute-start | bytes 884744 | tf_op jit(solution)/shard_map/ppermute | solution.py:396
  62.7 7.2 %collective-permute-start.20 = (bf16[192,256]{1,0:T(8,128)(2,1)S(1)}, bf16[192,256]{1,0:T(8,128)(2,1)S(1)}, u32[]{:S(2)}, u32[]{:S(2)}) collective-permute-start(bf16[192,256]{1,0:T(8,128)(2,1)S(1)} %slice.24), channel_id=1, source_target_pairs={{0,224},{8,232},{16,240},{24,248},{32,0},{40,8},{48,16},{56,24},{6... | collective-permute-start | bytes 294920 | tf_op jit(solution)/shard_map/ppermute | solution.py:390
  64.2 4.3 %collective-permute-start.17 = (bf16[128,256]{1,0:T(8,128)(2,1)S(1)}, bf16[128,256]{1,0:T(8,128)(2,1)S(1)}, u32[]{:S(2)}, u32[]{:S(2)}) collective-permute-start(bf16[128,256]{1,0:T(8,128)(2,1)S(1)} %slice.21), channel_id=1, source_target_pairs={{0,32},{8,40},{16,48},{24,56},{32,64},{40,72},{48,80},{56,88},{64,... | collective-permute-start | bytes 196616 | tf_op jit(solution)/shard_map/ppermute | solution.py:390
  65.6 9.0 %collective-permute-start.23 = (bf16[448,256]{1,0:T(8,128)(2,1)S(1)}, bf16[448,256]{1,0:T(8,128)(2,1)S(1)}, u32[]{:S(2)}, u32[]{:S(2)}) collective-permute-start(bf16[448,256]{1,0:T(8,128)(2,1)S(1)} %get-tuple-element.54), channel_id=1, source_target_pairs={{0,16},{8,24},{16,0},{24,8},{32,48},{40,56},{48,32},{56,40},{64,80... | collective-permute-start | bytes 688136 | tf_op jit(solution)/shard_map/ppermute | solution.py:393
  68.5 6.1 %collective-permute-start.18 = (bf16[128,256]{1,0:T(8,128)(2,1)S(1)}, bf16[128,256]{1,0:T(8,128)(2,1)S(1)}, u32[]{:S(2)}, u32[]{:S(2)}) collective-permute-start(bf16[128,256]{1,0:T(8,128)(2,1)S(1)} %collective-permute-done.17.ra_ref), channel_id=1, source_target_pairs={{0,8},{8,0},{16,24},{24,16},{32,40},{40,32},{48,56},{56,48},{64,72... | collective-permute-start | bytes 196616 | tf_op jit(solution)/shard_map/ppermute | solution.py:396
  70.0 4.7 %collective-permute-start.21 = (bf16[192,256]{1,0:T(8,128)(2,1)S(1)}, bf16[192,256]{1,0:T(8,128)(2,1)S(1)}, u32[]{:S(2)}, u32[]{:S(2)}) collective-permute-start(bf16[192,256]{1,0:T(8,128)(2,1)S(1)} %collective-permute-done.20.rb_ref), channel_id=1, source_target_pairs={{0,8},{8,0},{16,24},{24,16},{32,40},{40,32},{48,56},{56,48},{64,72... | collective-permute-start | bytes 294920 | tf_op jit(solution)/shard_map/ppermute | solution.py:396
